TPU v7x, 32 devices: a whole 2x2x4 slice. The times are simulated.
32 devices in a mesh: groups: 2 (over y), ctx: 4 (over z), head: 4 (over x, core).
Axes of the slice: x: 2, y: 2, z: 4, core: 2. Of those that a mesh axis runs over, the one named last changes fastest.
Arguments:
- query_rows: bfloat16 [3072, 3072], P(('groups', 'ctx', 'head')), parts along dimension 0, may hold values from -150 to 150
- key_rows: bfloat16 [3072, 3072], P(('groups', 'ctx', 'head')), parts along dimension 0, may hold values from -6 to 6
- value_rows: bfloat16 [3072, 3072], P(('groups', 'ctx', 'head')), parts along dimension 0, may hold values from -6 to 6
- tile_mask: int32 [8, 27], P(('groups', 'ctx')), parts along dimension 0, may hold values from 0 to 1, as said below
Outputs:
- attended: bfloat16 [3072, 3072], P(('groups', 'ctx', 'head')), parts along dimension 0
There are 2 independent parts, one for each index of `groups`. A program takes and returns all parts, laid end to end along the dimension named above; each array names one. Nothing has to cross between parts.
Inputs may be any that keep to these rules, and one draw needn't show every extreme that they name: `tile_mask`: entry o of row i is 1 only where the key tile of offset o lies inside the grid; entry 13 is always 1; a row has at most 4 ones, and some row has exactly 4.
All inputs are finite; a program needn't handle non-finite values.
Results may differ from a plain program's by a relative error of at most 0.0023.
Values may be sent and summed in bfloat16 or wider, within the bound.
No kernel may reach another device: no remote copies, remote signals or barrier semaphores. Data moves between devices by JAX's collectives and lax.ppermute only.
A program may use at most 64 MiB of HBM per device.

v0:
```python
import math

import jax
import jax.numpy as jnp
from jax import lax
from jax.sharding import PartitionSpec as P

HDIM = 128


def passed_along(block, axis, distance):
    devices = range(lax.axis_size(axis))
    route = [((i - distance) % len(devices), i) for i in devices]
    return lax.ppermute(block, axis, route)


def on_device(query_rows, key_rows, value_rows, tile_mask):
    cycle_size = lax.axis_size("ctx")
    grid_rows = max(2, cycle_size // 8)
    grid_cols = cycle_size // grid_rows
    query_local, key_local, value_local = (
        lax.all_to_all(query_rows, "head", split_axis=1, concat_axis=0, tiled=True),
        lax.all_to_all(key_rows, "head", split_axis=1, concat_axis=0, tiled=True),
        lax.all_to_all(value_rows, "head", split_axis=1, concat_axis=0, tiled=True),
    )
    feature_width = query_local.shape[1]
    head_count = feature_width // HDIM
    frames = tile_mask.shape[0]
    tile_len = query_local.shape[0] // frames
    key_value = jnp.stack([key_local, value_local]).reshape(2, frames, tile_len, feature_width)
    row_parts = [passed_along(key_value, "ctx", shift_by) for shift_by in (1, -1)]
    row_strip = jnp.stack([row_parts[0], key_value, row_parts[1]])
    column_parts = [
        passed_along(row_strip, "ctx", shift_by) for shift_by in (grid_cols, -grid_cols)
    ]
    window = jnp.stack([column_parts[0], row_strip, column_parts[1]])
    key_tiles = window[:, :, 0].reshape(9 * frames, tile_len, feature_width)
    value_tiles = window[:, :, 1].reshape(9 * frames, tile_len, feature_width)
    kept_mask = tile_mask == 1
    first_offset = 9
    slot_count = 9
    slot_order = jnp.arange(first_offset, first_offset + slot_count, dtype=jnp.int32)[None, :]
    slot_kept = kept_mask[:, first_offset : first_offset + slot_count]
    frame_ids = jnp.arange(frames, dtype=jnp.int32)[:, None]
    source_frame = jnp.clip(frame_ids + slot_order // 9 - 1, 0, frames - 1)
    source = slot_order % 9 * frames + source_frame
    kept_cols = jnp.repeat(slot_kept, tile_len, axis=1)[:, None, :]
    score_scale = 1.0 / math.sqrt(HDIM)

    def one_head(head_index):
        column_start = head_index * HDIM
        key_head = lax.dynamic_slice_in_dim(key_tiles, column_start, HDIM, 2)
        value_head = lax.dynamic_slice_in_dim(value_tiles, column_start, HDIM, 2)
        query_head = lax.dynamic_slice_in_dim(query_local, column_start, HDIM, 1).reshape(
            frames, tile_len, HDIM
        )
        picked_keys = jnp.take(key_head, source, axis=0).reshape(
            frames, slot_count * tile_len, HDIM
        )
        picked_values = jnp.take(value_head, source, axis=0).reshape(
            frames, slot_count * tile_len, HDIM
        )
        scores = (
            jnp.einsum("fqd,fkd->fqk", query_head, picked_keys, preferred_element_type=jnp.float32)
            * score_scale
        )
        row_peak = jnp.max(jnp.where(kept_cols, scores, -jnp.inf), axis=2, keepdims=True)
        weight = jnp.exp(jnp.where(kept_cols, scores - row_peak, -jnp.inf))
        row_total = jnp.sum(weight, axis=2, keepdims=True)
        rounded = weight.astype(jnp.bfloat16)
        mixed = jnp.einsum(
            "fqk,fkd->fqd", rounded, picked_values, preferred_element_type=jnp.float32
        )
        return (mixed / row_total).astype(jnp.bfloat16)

    result = lax.map(one_head, jnp.arange(head_count, dtype=jnp.int32))
    result = jnp.transpose(result, (1, 2, 0, 3)).reshape(frames * tile_len, feature_width)
    return lax.all_to_all(result, "head", split_axis=0, concat_axis=1, tiled=True)


def solution(mesh):
    placed = (
        P(("groups", "ctx", "head"), None),
        P(("groups", "ctx", "head"), None),
        P(("groups", "ctx", "head"), None),
        P(("groups", "ctx"), None),
    )
    return jax.shard_map(
        on_device,
        mesh=mesh,
        in_specs=placed,
        out_specs=P(("groups", "ctx", "head"), None),
        check_vma=False,
    )
```

profile of v0, /device:TPU:0, one launch (start us, length us, event | category | flops | bytes accessed | tf_op | source)
XLA Modules:
  0.0 327.5 jit_solution(2252575000279086143)
XLA Ops:
  0.0 1.9 copy.44
  1.9 4.2 %all-to-all-start.1 = ((bf16[96,4,768]{2,0,1:T(8,128)(2,1)}), bf16[96,4,768]{2,0,1:T(8,128)(2,1)S(1)}, u32[]{:S(2)}, u32[]{:S(2)}) async-start(bf16[96,4,768]{2,0,1:T(8,128)(2,1)} %bitcast.57), calls=%async_computation.1 | async-start | bytes 1179648 | tf_op jit(solution)/shard_map/all_to_all | solution.py:23
  7.3 8.4 %all-to-all-done.1 = bf16[96,4,768]{2,0,1:T(8,128)(2,1)S(1)} async-done(((bf16[96,4,768]{2,0,1:T(8,128)(2,1)}), bf16[96,4,768]{2,0,1:T(8,128)(2,1)S(1)}, u32[]{:S(2)}, u32[]{:S(2)}) %all-to-all-start.1) | async-done | bytes 589856 | tf_op jit(solution)/shard_map/all_to_all | solution.py:23
  15.7 11.9 %all_to_all.70 = bf16[96,4,768]{2,0,1:T(8,128)(2,1)S(1)} all-to-all(bf16[96,4,768]{2,0,1:T(8,128)(2,1)S(1)} %bitcast.84), channel_id=1, replica_groups=mesh['groups'=2,'ctx'=4,'head'=4] {'head'}, dimensions={1} | all-to-all | bytes 1179648 | tf_op jit(solution)/shard_map/all_to_all | solution.py:24
  27.7 2.3 collective-permute-start
  30.0 2.1 collective-permute-start.1
  32.1 26.8 %collective-permute-done = bf16[2,1,384,768]{3,2,0,1:T(8,128)(2,1)S(1)} collective-permute-done((bf16[2,1,384,768]{3,2,0,1:T(8,128)(2,1)S(1)}, bf16[2,1,384,768]{3,2,0,1:T(8,128)(2,1)S(1)}, u32[]{:S(2)}, u32[]{:S(2)}) %collective-permute-start) | collective-permute-done | bytes 1179680 | tf_op jit(solution)/shard_map/ppermute | solution.py:14
  58.9 23.7 %collective-permute-done.1 = bf16[2,1,384,768]{3,2,0,1:T(8,128)(2,1)S(1)} collective-permute-done((bf16[2,1,384,768]{3,2,0,1:T(8,128)(2,1)S(1)}, bf16[2,1,384,768]{3,2,0,1:T(8,128)(2,1)S(1)}, u32[]{:S(2)}, u32[]{:S(2)}) %collective-permute-start.1) | collective-permute-done | bytes 1179680 | tf_op jit(solution)/shard_map/ppermute | solution.py:14
  82.7 2.0 fusion.32
  86.9 4.2 %all-to-all-start = ((bf16[96,4,768]{2,0,1:T(8,128)(2,1)}), bf16[96,4,768]{2,0,1:T(8,128)(2,1)}, u32[]{:S(2)}, u32[]{:S(2)}) async-start(bf16[96,4,768]{2,0,1:T(8,128)(2,1)} %bitcast.83), calls=%async_computation | async-start | bytes 1179648 | tf_op jit(solution)/shard_map/all_to_all | solution.py:22
  91.2 148.5 %collective-permute-done.2 = bf16[3,2,1,384,768]{4,3,1,0,2:T(8,128)(2,1)} collective-permute-done((bf16[3,2,1,384,768]{4,3,1,0,2:T(8,128)(2,1)}, bf16[3,2,1,384,768]{4,3,1,0,2:T(8,128)(2,1)}, u32[]{:S(2)}, u32[]{:S(2)}) %collective-permute-start.2) | collective-permute-done | bytes 3538976 | tf_op jit(solution)/shard_map/ppermute | solution.py:14
  239.6 8.4 %pad_maximum_fusion = bf16[3,3,2,1,384,768]{5,4,2,1,3,0:T(8,128)(2,1)} fusion(bf16[1,3,2,1,384,768]{5,4,2,1,3,0:T(8,128)(2,1)} %bitcast.11, bf16[1,3,2,1,384,768]{5,4,2,1,3,0:T(8,128)(2,1)S(1)} %get-tuple-element.112), kind=kLoop, calls=%fused_computation.36 | loop fusion | flops 10616832 | bytes 17694720 | tf_op jit(solution)/shard_map/stack | solution.py:36
  248.0 8.9 %fusion.36 = (bf16[3,3,1,1,384,768]{5,4,2,1,3,0:T(8,128)(2,1)}, bf16[3,3,1,1,384,768]{5,4,2,1,3,0:T(8,128)(2,1)}) fusion(bf16[3,3,2,1,384,768]{5,4,2,1,3,0:T(8,128)(2,1)} %pad_maximum_fusion), kind=kLoop, calls=%fused_computation.48 | loop fusion | bytes 21233664 | tf_op jit(solution)/shard_map/slice | solution.py:38
  256.9 55.6 %while.12 = (s32[]{:T(128)}, bf16[6,1,384,128]{3,2,1,0:T(8,128)(2,1)}, s32[6]{0:T(128)S(1)}, bf16[384,768]{1,0:T(8,128)(2,1)}, bf16[9,384,768]{2,1,0:T(8,128)(2,...) while((s32[]{:T(128)}, ...), condition=%wide.region_3.5_spmd.clone.clone, body=%wide.region_0.4_spmd.clone.clone.sunk | while | flops 692404736 | bytes 28541528 | solution.py:76
  261.6 1.9 select_reduce_fusion.2
  264.6 1.6 fusion.50
  270.9 1.9 select_reduce_fusion.2
  280.1 1.9 select_reduce_fusion.2
  289.4 1.9 select_reduce_fusion.2
  292.4 1.6 fusion.50
  298.7 1.9 select_reduce_fusion.2
  307.9 1.9 select_reduce_fusion.2
  310.9 1.6 fusion.50
  314.7 11.9 %all_to_all.71 = bf16[4,96,768]{2,1,0:T(8,128)(2,1)S(1)} all-to-all(bf16[4,96,768]{2,1,0:T(8,128)(2,1)S(1)} %all_to_all.62), channel_id=1, replica_groups=mesh['groups'=2,'ctx'=4,'head'=4] {'head'}, dimensions={0} | all-to-all | bytes 1179648 | tf_op jit(solution)/shard_map/all_to_all | solution.py:78
  (85 shorter events, 42.0 us)
Async XLA Ops:
  1.9 13.8 %all-to-all-start.1 = ((bf16[96,4,768]{2,0,1:T(8,128)(2,1)}), bf16[96,4,768]{2,0,1:T(8,128)(2,1)S(1)}, u32[]{:S(2)}, u32[]{:S(2)}) async-start(bf16[96,4,768]{2,0,1:T(8,128)(2,1)} %bitcast.57), calls=%async_computation.1 | async-start | bytes 1179648 | tf_op jit(solution)/shard_map/all_to_all | solution.py:23
  27.7 31.2 %collective-permute-start = (bf16[2,1,384,768]{3,2,0,1:T(8,128)(2,1)S(1)}, bf16[2,1,384,768]{3,2,0,1:T(8,128)(2,1)S(1)}, u32[]{:S(2)}, u32[]{:S(2)}) collective-permute-start(bf16[2,1,384,768]{3,2,0,1:T(8,128)(2,1)S(1)} %get-tuple-element.115), channel_id=1, source_target_pairs={{12,0},{0,4},{4,8},{8,12},{13,1},{1,5},{5,9},{9,13},{14,2},{2,6},{... | collective-permute-start | bytes 3538952 | tf_op jit(solution)/shard_map/ppermute | solution.py:14
  30.0 52.6 %collective-permute-start.1 = (bf16[2,1,384,768]{3,2,0,1:T(8,128)(2,1)S(1)}, bf16[2,1,384,768]{3,2,0,1:T(8,128)(2,1)S(1)}, u32[]{:S(2)}, u32[]{:S(2)}) collective-permute-start(bf16[2,1,384,768]{3,2,0,1:T(8,128)(2,1)S(1)} %get-tuple-element.115), channel_id=1, source_target_pairs={{4,0},{8,4},{12,8},{0,12},{5,1},{9,5},{13,9},{1,13},{6,2},{10,6},{... | collective-permute-start | bytes 3538952 | tf_op jit(solution)/shard_map/ppermute | solution.py:14
  82.7 3.3 %copy-start = (bf16[96,3072]{1,0:T(8,128)(2,1)S(1)}, bf16[96,3072]{1,0:T(8,128)(2,1)}, u32[]{:S(2)}) copy-start(bf16[96,3072]{1,0:T(8,128)(2,1)} %param.8) | copy-start | bytes 1769476
  82.7 8.4 %copy-start.1 = (s32[1,27]{1,0:T(1,128)S(1)}, s32[1,27]{1,0:T(1,128)}, u32[]{:S(2)}) copy-start(s32[1,27]{1,0:T(1,128)} %param.11) | copy-start | bytes 328
  84.7 154.9 %collective-permute-start.2 = (bf16[3,2,1,384,768]{4,3,1,0,2:T(8,128)(2,1)}, bf16[3,2,1,384,768]{4,3,1,0,2:T(8,128)(2,1)}, u32[]{:S(2)}, u32[]{:S(2)}) collective-permute-start(bf16[3,2,1,384,768]{4,3,1,0,2:T(8,128)(2,1)} %get-tuple-element.113), channel_id=1, source_target_pairs={{8,0},{12,4},{0,8},{4,12},{9,1},{13,5},{1,9},{5,13},{10,2},{14,6},... | collective-permute-start | bytes 10616840 | tf_op jit(solution)/shard_map/ppermute | solution.py:14
  86.9 170.0 %all-to-all-start = ((bf16[96,4,768]{2,0,1:T(8,128)(2,1)}), bf16[96,4,768]{2,0,1:T(8,128)(2,1)}, u32[]{:S(2)}, u32[]{:S(2)}) async-start(bf16[96,4,768]{2,0,1:T(8,128)(2,1)} %bitcast.83), calls=%async_computation | async-start | bytes 1179648 | tf_op jit(solution)/shard_map/all_to_all | solution.py:22
where the time goes:
time: 328 us; the launch traced here: 327 us
  waiting for transfers between devices  207 us (63%)
  local copies, waits for them, and re-layouts  38.3 us (12%)
  blocking collectives  23.8 us (7%)
  matrix products  21.1 us (6%)
  other arithmetic  18.6 us (6%)
  starting transfers between devices  14.1 us (4%)
  loops' own time  4.07 us (1%)
    ppermute x3, waiting for transfers between devices, passed_along(): return lax.ppermute(block, axis, route)  199 us
    all_to_all x1, blocking collectives, on_device(): lax.all_to_all(result, 'head', split_axis=0, concat_axis=1, tiled=True)  11.9 us
    all_to_all x1, blocking collectives, on_device(): lax.all_to_all(value_rows, 'head', split_axis=1, concat_axis=0, tiled=True)  11.9 us
    dot_general x6, matrix products, one_head(): jnp.einsum('fqd,fkd->fqk', query_head, picked_keys, preferred_element_typ...  11.2 us
    another operation x2, other arithmetic, on_device(): window = jnp.stack([column_parts[0], row_strip, column_parts[1]])  10.4 us
    dot_general x6, matrix products, one_head(): jnp.einsum('fqk,fkd->fqd', rounded, picked_values, preferred_element_type...  9.83 us
    dynamic_slice x6, local copies, waits for them, and re-layouts, one_head(): value_head = lax.dynamic_slice_in_dim(value_tiles, column_start, HDIM, 2)  9.42 us
    slice x1, local copies, waits for them, and re-layouts, on_device(): value_tiles = window[:, :, 1].reshape(9 * frames, tile_len, feature_width)  8.9 us
  transfers between devices with their start and end apart: 5, of which 4 were waited for; matrix products, arithmetic and copies ran while one was open for 6% of the time, Pallas kernels for 0%

commit v1 on v0

--- a/solution.py
+++ b/solution.py
@@ -1,9 +1,13 @@
+import functools
 import math
 
 import jax
 import jax.numpy as jnp
 from jax import lax
-from jax.sharding import PartitionSpec as P
+from jax.experimental import pallas as pl
+from jax.experimental.pallas import tpu as pltpu
+from jax.sharding import Mesh, PartitionSpec as P
+
 
 HDIM = 128
 
@@ -78,17 +82,265 @@
     return lax.all_to_all(result, "head", split_axis=0, concat_axis=1, tiled=True)
 
 
+AXES = ("pair", "mate", "head")
+AHEAD = (1, 3, 0, 2)
+BEHIND = (2, 0, 3, 1)
+ACROSS = (3, 2, 1, 0)
+MASKED = -1e30
+FACTOR = math.log2(math.e) / math.sqrt(HDIM)
+
+
+def flipped(index, bits, size):
+    out, step = 0, 1
+    while step < size:
+        bit = (index // step) % 2
+        out = out + step * (1 - bit if (bits // step) % 2 else bit)
+        step *= 2
+    return out
+
+
+def columns_of(mate, l, heads, width):
+    group = mate * heads + flipped(lax.axis_index("head"), l, heads)
+    return pl.ds(pl.multiple_of(group * width, 128), width)
+
+
+def copy_all(copies, sem):
+    copies = [pltpu.make_async_copy(a, b, sem.at[n]) for n, (a, b) in enumerate(copies)]
+    for copy in copies:
+        copy.start()
+    for copy in copies:
+        copy.wait()
+
+
+def cut_ahead_kernel(heads, width, k_ref, v_ref, *rest):
+    outs, sem = rest[:-1], rest[-1]
+    copies = []
+    for l, out in enumerate(outs):
+        cols = columns_of(1 - lax.axis_index("pair"), l, heads, width)
+        for n, part in enumerate((k_ref, v_ref)):
+            copies.append((part.at[:, cols], out.at[:, n * width : (n + 1) * width]))
+    copy_all(copies, sem)
+
+
+def cut_rest_kernel(heads, width, q_ref, k_ref, v_ref, *rest):
+    outs, sem = rest[:-1], rest[-1]
+    own = lax.axis_index("mate")
+    mates = (own, 1 - own, lax.axis_index("pair"))
+    copies = []
+    for i, out in enumerate(outs[: 3 * heads]):
+        cols = columns_of(mates[i // heads], i % heads, heads, width)
+        for n, part in enumerate((k_ref, v_ref)):
+            copies.append((part.at[:, cols], out.at[:, n * width : (n + 1) * width]))
+    for s, out in enumerate(outs[3 * heads :]):
+        cols = columns_of(mates[s // heads], s % heads, heads, width)
+        copies.append((q_ref.at[:, cols], out))
+    copy_all(copies, sem)
+
+
+def cut_call(kernel, inputs, key_values, queries, heads, width):
+    rows = inputs[0].shape[0]
+    shapes = [jax.ShapeDtypeStruct((rows, 2 * width), jnp.bfloat16)] * key_values
+    shapes += [jax.ShapeDtypeStruct((rows, width), jnp.bfloat16)] * queries
+    return pl.pallas_call(
+        functools.partial(kernel, heads, width),
+        out_shape=shapes,
+        in_specs=[pl.BlockSpec(memory_space=pltpu.VMEM)] * len(inputs),
+        out_specs=[pl.BlockSpec(memory_space=pl.ANY)] * len(shapes),
+        scratch_shapes=[pltpu.SemaphoreType.DMA((2 * key_values + queries,))],
+    )(*inputs)
+
+
+def tile_bias(masks, own, key_blocks, tile):
+    z = lax.axis_index("pair") * 2 + lax.axis_index("mate")
+
+    def place(block):
+        p = (block + 3) % 4
+        return p // 2, p % 2
+
+    row, col = place(flipped(z, own, 4))
+    lane_tile = lax.broadcasted_iota(jnp.int32, (1, len(key_blocks) * tile), 1) // tile
+    bias = jnp.zeros(lane_tile.shape, jnp.float32)
+    for n, block in enumerate(key_blocks):
+        key_row, key_col = place(block)
+        offset = 9 + 3 * (key_row - row + 1) + (key_col - col + 1)
+        dropped = masks[own][0, offset] != 1
+        bias = jnp.where((lane_tile == n) & dropped, MASKED, bias)
+    return bias
+
+
+def key_blocks():
+    pair, mate = lax.axis_index("pair"), lax.axis_index("mate")
+    z = 2 * pair + mate
+    return z, 2 * (1 - mate) + pair, 3 - z, 2 * mate + 1 - pair
+
+
+def softmax_part(q, k, v, bias):
+    scores = lax.dot_general(q, k, (((1,), (1,)), ((), ())), preferred_element_type=jnp.float32)
+    scores = scores + bias
+    peak = jnp.max(scores, axis=1, keepdims=True)
+    weight = jnp.exp2((scores - peak) * FACTOR)
+    total = jnp.sum(weight, axis=1, keepdims=True)
+    mixed = jnp.dot(weight.astype(jnp.bfloat16), v, preferred_element_type=jnp.float32)
+    return peak, total, mixed
+
+
+def first_kernel(heads, width, *refs):
+    masks, refs = refs[:2], refs[2:]
+    queries, refs = refs[: 2 * heads], refs[2 * heads :]
+    pieces, refs = refs[: 3 * heads], refs[3 * heads :]
+    q_out, stat_out, mixed_out, kbuf, vbuf = refs
+    rows = queries[0].shape[0]
+    tile = heads * rows
+    for s, piece in enumerate(queries):
+        q_out[s * rows : (s + 1) * rows, :] = piece[...]
+    for s, piece in enumerate(pieces):
+        kbuf[s * rows : (s + 1) * rows, :] = piece[:, :width]
+        vbuf[s * rows : (s + 1) * rows, :] = piece[:, width:]
+    for own in range(2):
+        bias = tile_bias(masks, own, key_blocks()[:3], tile)
+        at = slice(own * tile, (own + 1) * tile)
+        for h in range(width // HDIM):
+            cols = slice(h * HDIM, (h + 1) * HDIM)
+            peak, total, mixed = softmax_part(q_out[at, cols], kbuf[:, cols], vbuf[:, cols], bias)
+            stat_out[at, 2 * h : 2 * h + 1] = peak
+            stat_out[at, 2 * h + 1 : 2 * h + 2] = total
+            mixed_out[at, cols] = mixed
+
+
+def last_kernel(heads, width, *refs):
+    masks, refs = refs[:2], refs[2:]
+    q_ref, stat_ref, mixed_ref, refs = refs[0], refs[1], refs[2], refs[3:]
+    pieces, refs = refs[:heads], refs[heads:]
+    outs, kbuf, vbuf = refs[: 2 * heads], refs[2 * heads], refs[2 * heads + 1]
+    rows = pieces[0].shape[0]
+    tile = heads * rows
+    for s, piece in enumerate(pieces):
+        kbuf[s * rows : (s + 1) * rows, :] = piece[:, :width]
+        vbuf[s * rows : (s + 1) * rows, :] = piece[:, width:]
+    for own in range(2):
+        bias = tile_bias(masks, own, key_blocks()[3:], tile)
+        at = slice(own * tile, (own + 1) * tile)
+        for h in range(width // HDIM):
+            cols = slice(h * HDIM, (h + 1) * HDIM)
+            peak, total, mixed = softmax_part(q_ref[at, cols], kbuf[:, cols], vbuf[:, cols], bias)
+            old_peak = stat_ref[at, 2 * h : 2 * h + 1]
+            old_total = stat_ref[at, 2 * h + 1 : 2 * h + 2]
+            top = jnp.maximum(peak, old_peak)
+            new_share = jnp.exp2((peak - top) * FACTOR)
+            old_share = jnp.exp2((old_peak - top) * FACTOR)
+            total = total * new_share + old_total * old_share
+            mixed = mixed * new_share + mixed_ref[at, cols] * old_share
+            result = (mixed / total).astype(jnp.bfloat16)
+            for n in range(heads):
+                outs[own * heads + n][:, cols] = result[n * rows : (n + 1) * rows]
+
+
+def attend_first(masks, queries, pieces, heads, width):
+    rows = pieces[0].shape[0]
+    tile = heads * rows
+    vmem = pl.BlockSpec(memory_space=pltpu.VMEM)
+    return pl.pallas_call(
+        functools.partial(first_kernel, heads, width),
+        out_shape=[
+            jax.ShapeDtypeStruct((2 * tile, width), jnp.bfloat16),
+            jax.ShapeDtypeStruct((2 * tile, 128), jnp.float32),
+            jax.ShapeDtypeStruct((2 * tile, width), jnp.float32),
+        ],
+        in_specs=[pl.BlockSpec(memory_space=pltpu.SMEM)] * 2
+        + [vmem] * (len(queries) + len(pieces)),
+        out_specs=[vmem] * 3,
+        scratch_shapes=[pltpu.VMEM((3 * tile, width), jnp.bfloat16)] * 2,
+        name="first",
+    )(*masks, *queries, *pieces)
+
+
+def attend_last(masks, carried, pieces, heads, width):
+    rows = pieces[0].shape[0]
+    tile = heads * rows
+    vmem = pl.BlockSpec(memory_space=pltpu.VMEM)
+    return pl.pallas_call(
+        functools.partial(last_kernel, heads, width),
+        out_shape=[jax.ShapeDtypeStruct((rows, width), jnp.bfloat16)] * (2 * heads),
+        in_specs=[pl.BlockSpec(memory_space=pltpu.SMEM)] * 2 + [vmem] * (3 + len(pieces)),
+        out_specs=[vmem] * (2 * heads),
+        scratch_shapes=[pltpu.VMEM((tile, width), jnp.bfloat16)] * 2,
+        name="last",
+    )(*masks, *carried, *pieces)
+
+
+def join_kernel(heads, width, *refs):
+    pieces, out = refs[:-1], refs[-1]
+    own = lax.axis_index("mate")
+    for s, piece in enumerate(pieces):
+        mate = 1 - own if s >= heads else own
+        out[:, columns_of(mate, s % heads, heads, width)] = piece[...]
+
+
+def join(pieces, heads, width):
+    rows = pieces[0].shape[0]
+    vmem = pl.BlockSpec(memory_space=pltpu.VMEM)
+    return pl.pallas_call(
+        functools.partial(join_kernel, heads, width),
+        out_shape=jax.ShapeDtypeStruct((rows, 2 * heads * width), jnp.bfloat16),
+        in_specs=[vmem] * len(pieces),
+        out_specs=vmem,
+        name="join",
+    )(*pieces)
+
+
+def moved(block, pattern, l, heads):
+    route = [
+        (z * heads + h, pattern[z] * heads + (h ^ l)) for z in range(4) for h in range(heads)
+    ]
+    return lax.ppermute(block, AXES, route)
+
+
+OWN, MATE = (0, 1, 2, 3), (1, 0, 3, 2)
+
+
+def on_device_square(query_rows, key_rows, value_rows, tile_mask):
+    heads = lax.axis_size("head")
+    width = query_rows.shape[1] // (2 * heads)
+    some = range(heads)
+    sent = cut_call(cut_ahead_kernel, (key_rows, value_rows), heads, 0, heads, width)
+    ahead = [moved(sent[l], AHEAD, l, heads) for l in some]
+    inputs = (query_rows, key_rows, value_rows)
+    rest = cut_call(cut_rest_kernel, inputs, 3 * heads, 2 * heads, heads, width)
+    asked = rest[3 * heads :]
+    queries = [asked[0]] + [
+        moved(asked[s], MATE if s >= heads else OWN, s % heads, heads)
+        for s in range(1, 2 * heads)
+    ]
+    own = [rest[0]] + [moved(rest[l], OWN, l, heads) for l in some[1:]]
+    across = [moved(rest[heads + l], ACROSS, l, heads) for l in some]
+    behind = [moved(rest[2 * heads + l], BEHIND, l, heads) for l in some]
+    masks = (tile_mask, moved(tile_mask, MATE, 0, heads))
+    carried = attend_first(masks, queries, own + ahead + across, heads, width)
+    parts = attend_last(masks, carried, behind, heads, width)
+    order = [s for s in range(heads, 2 * heads)] + list(some[1:])
+    back = {0: parts[0]}
+    for s in order:
+        back[s] = moved(parts[s], MATE if s >= heads else OWN, s % heads, heads)
+    return join([back[s] for s in range(2 * heads)], heads, width)
+
+
 def solution(mesh):
-    placed = (
-        P(("groups", "ctx", "head"), None),
-        P(("groups", "ctx", "head"), None),
-        P(("groups", "ctx", "head"), None),
-        P(("groups", "ctx"), None),
-    )
+    groups, ctx, heads = (mesh.shape[name] for name in ("groups", "ctx", "head"))
+    if ctx == 4 and heads & (heads - 1) == 0:
+        square = Mesh(mesh.devices.reshape(groups, 2, 2, heads), ("groups",) + AXES)
+        rows = P(("groups",) + AXES, None)
+        return jax.shard_map(
+            on_device_square,
+            mesh=square,
+            in_specs=(rows, rows, rows, P(("groups", "pair", "mate"), None)),
+            out_specs=rows,
+            check_vma=False,
+        )
+    rows = P(("groups", "ctx", "head"), None)
     return jax.shard_map(
         on_device,
         mesh=mesh,
-        in_specs=placed,
-        out_specs=P(("groups", "ctx", "head"), None),
+        in_specs=(rows, rows, rows, P(("groups", "ctx"), None)),
+        out_specs=rows,
         check_vma=False,
     )

time: 328 us -> 102 us (0.31)
  waiting for transfers between devices: 207 us -> 13.2 us
  starting transfers between devices: 14.1 us -> 62.4 us
  local copies, waits for them, and re-layouts: 38.3 us -> 1.96 us
  blocking collectives: 23.8 us -> 0 us
  Pallas kernels: 0 us -> 23.7 us
  matrix products: 21.1 us -> 0 us
  other arithmetic: 18.6 us -> 0 us
  loops' own time: 4.07 us -> 0 us
    ppermute x3 -> x30, waiting for transfers between devices: 199 us -> 13.2 us  [moved(): return lax.ppermute(block, AXES, route)]
    ppermute x3 -> x30, starting transfers between devices: 5.73 us -> 62.4 us  [moved(): return lax.ppermute(block, AXES, route)]
    all_to_all x2 -> x0, blocking collectives: 23.8 us -> none  [the longest x1 11.9 us: on_device(): lax.all_to_all(result, 'head', split_axis=0, concat_axis=1, tiled=True)]
    pallas_call x0 -> x5, Pallas kernels: none -> 23.7 us  [the longest x1 8.52 us: attend_last(): pl.pallas_call(functools.partial(last_kernel, heads, width), out_shape=[j...]
    dot_general x12 -> x0, matrix products: 21.1 us -> none  [the longest x6 11.2 us: one_head(): jnp.einsum('fqd,fkd->fqk', query_head, picked_keys, preferred_element_typ...]
    dynamic_slice x12 -> x0, local copies, waits for them, and re-layouts: 13.2 us -> none  [the longest x6 9.42 us: one_head(): value_head = lax.dynamic_slice_in_dim(value_tiles, column_start, HDIM, 2)]
    another operation x3 -> x0, other arithmetic: 10.6 us -> none  [the longest x2 10.4 us: on_device(): window = jnp.stack([column_parts[0], row_strip, column_parts[1]])]
    slice x2 -> x0, local copies, waits for them, and re-layouts: 8.98 us -> none  [the longest x1 8.9 us: on_device(): value_tiles = window[:, :, 1].reshape(9 * frames, tile_len, feature_width)]
  transfers between devices with their start and end apart: 5 -> 30, of which waited for: 4 -> 8; matrix products, arithmetic and copies ran while one was open for 6% -> 0% of each run, Pallas kernels for 0% -> 10%
where the time goes in v1:
time: 102 us
  starting transfers between devices  62.4 us (61%)
  Pallas kernels  23.7 us (23%)
  waiting for transfers between devices  13.2 us (13%)
  local copies, waits for them, and re-layouts  1.96 us (2%)
    ppermute x30, starting transfers between devices, moved(): return lax.ppermute(block, AXES, route)  62.4 us
    ppermute x30, waiting for transfers between devices, moved(): return lax.ppermute(block, AXES, route)  13.2 us
    pallas_call x1, Pallas kernels, attend_last(): pl.pallas_call(functools.partial(last_kernel, heads, width), out_shape=[j...  8.52 us
    pallas_call x1, Pallas kernels, attend_first(): pl.pallas_call(functools.partial(first_kernel, heads, width), out_shape=[...  7.91 us
    pallas_call x2, Pallas kernels, cut_call(): pl.pallas_call(functools.partial(kernel, heads, width), out_shape=shapes,...  5.24 us
  transfers between devices with their start and end apart: 30, of which 8 were waited for; matrix products, arithmetic and copies ran while one was open for 0% of the time, Pallas kernels for 10%

profile of v1, /device:TPU:0, one launch (start us, length us, event | category | flops | bytes accessed | tf_op | source)
XLA Modules:
  0.0 101.6 jit_solution(9826755396204097677)
XLA Ops:
  0.0 3.1 %shard_map.46 = (bf16[96,768]{1,0:T(8,128)(2,1)}, bf16[96,768]{1,0:T(8,128)(2,1)}, bf16[96,768]{1,0:T(8,128)(2,1)}, bf16[96,768]{1,0:T(8,128)(2,1)}, bf16[96,768...) custom-call(bf16[96,3072]{1,0:T(8,128)(2,1)} %q_ref.1, ...), custom_call_target="tpu_custom_call" | custom-call | tf_op jit(solution)/shard_map/pallas_call | solution.py:144
  3.7 2.6 %collective-permute-start.2 = (bf16[96,384]{1,0:T(8,128)(2,1)}, bf16[96,384]{1,0:T(8,128)(2,1)S(1)}, u32[]{:S(2)}, u32[]{:S(2)}) collective-permute-start(bf16[96,384]{1,0:T(8,128)(2,1)} %get-tuple-element.42), channel_id=1, source_target_pairs={{0,2},{1,3},{2,0},{3,1},{4,6},{5,7},{6,4},{7,5},{8,10},{9,11},{10,... | collective-permute-start | bytes 221192 | tf_op jit(solution)/shard_map/ppermute | solution.py:295
  6.3 1.8 %collective-permute-start = (s32[1,27]{1,0:T(1,128)S(1)}, s32[1,27]{1,0:T(1,128)S(1)}, u32[]{:S(2)}, u32[]{:S(2)}) collective-permute-start(s32[1,27]{1,0:T(1,128)S(1)} %copy-done.29), channel_id=1, source_target_pairs={{0,4},{1,5},{2,6},{3,7},{4,0},{5,1},{6,2},{7,3},{8,12},{9,13},{10,... | collective-permute-start | bytes 332 | tf_op jit(solution)/shard_map/ppermute | solution.py:295
  8.4 1.5 %collective-permute-done.refs_1_ = s32[1,27]{1,0:T(1,128)S(1)} collective-permute-done((s32[1,27]{1,0:T(1,128)S(1)}, s32[1,27]{1,0:T(1,128)S(1)}, u32[]{:S(2)}, u32[]{:S(2)}) %collective-permute-start) | collective-permute-done | bytes 140 | tf_op jit(solution)/shard_map/ppermute | solution.py:295
  10.9 1.9 %collective-permute-start.6 = (bf16[96,384]{1,0:T(8,128)(2,1)}, bf16[96,384]{1,0:T(8,128)(2,1)S(1)}, u32[]{:S(2)}, u32[]{:S(2)}) collective-permute-start(bf16[96,384]{1,0:T(8,128)(2,1)} %get-tuple-element.46), channel_id=1, source_target_pairs={{0,6},{1,7},{2,4},{3,5},{4,2},{5,3},{6,0},{7,1},{8,14},{9,15},{10,... | collective-permute-start | bytes 221192 | tf_op jit(solution)/shard_map/ppermute | solution.py:295
  14.1 2.1 %shard_map.47 = (bf16[96,768]{1,0:T(8,128)(2,1)}, bf16[96,768]{1,0:T(8,128)(2,1)}, bf16[96,768]{1,0:T(8,128)(2,1)}, bf16[96,768]{1,0:T(8,128)(2,1)}) custom-call(bf16[96,3072]{1,0:T(8,128)(2,1)} %k_ref.3, bf16[96,3072]{1,0:T(8,128)(2,1)} %v_ref.3), custom_call_target="tpu_custom_call" | custom-call | tf_op jit(solution)/shard_map/pallas_call | solution.py:144
  16.7 2.3 %collective-permute-start.12 = (bf16[96,768]{1,0:T(8,128)(2,1)}, bf16[96,768]{1,0:T(8,128)(2,1)S(1)}, u32[]{:S(2)}, u32[]{:S(2)}) collective-permute-start(bf16[96,768]{1,0:T(8,128)(2,1)} %get-tuple-element.53), channel_id=1, source_target_pairs={{0,5},{1,4},{2,7},{3,6},{4,13},{5,12},{6,15},{7,14},{8,1},{9,0},{1... | collective-permute-start | bytes 442376 | tf_op jit(solution)/shard_map/ppermute | solution.py:295
  19.0 2.0 %collective-permute-start.13 = (bf16[96,768]{1,0:T(8,128)(2,1)}, bf16[96,768]{1,0:T(8,128)(2,1)S(1)}, u32[]{:S(2)}, u32[]{:S(2)}) collective-permute-start(bf16[96,768]{1,0:T(8,128)(2,1)} %get-tuple-element.54), channel_id=1, source_target_pairs={{0,6},{1,7},{2,4},{3,5},{4,14},{5,15},{6,12},{7,13},{8,2},{9,3},{1... | collective-permute-start | bytes 442376 | tf_op jit(solution)/shard_map/ppermute | solution.py:295
  22.1 2.1 %collective-permute-done.11.refs_14_ = bf16[96,768]{1,0:T(8,128)(2,1)S(1)} collective-permute-done((bf16[96,768]{1,0:T(8,128)(2,1)}, bf16[96,768]{1,0:T(8,128)(2,1)S(1)}, u32[]{:S(2)}, u32[]{:S(2)}) %collective-permute-start.11) | collective-permute-done | bytes 147488 | tf_op jit(solution)/shard_map/ppermute | solution.py:295
  25.7 2.9 %collective-permute-start.10 = (bf16[96,768]{1,0:T(8,128)(2,1)}, bf16[96,768]{1,0:T(8,128)(2,1)S(1)}, u32[]{:S(2)}, u32[]{:S(2)}) collective-permute-start(bf16[96,768]{1,0:T(8,128)(2,1)} %get-tuple-element.51), channel_id=1, source_target_pairs={{0,3},{1,2},{2,1},{3,0},{4,7},{5,6},{6,5},{7,4},{8,11},{9,10},{10,... | collective-permute-start | bytes 442376 | tf_op jit(solution)/shard_map/ppermute | solution.py:295
  28.6 3.0 %collective-permute-done.13.refs_16_ = bf16[96,768]{1,0:T(8,128)(2,1)S(1)} collective-permute-done((bf16[96,768]{1,0:T(8,128)(2,1)}, bf16[96,768]{1,0:T(8,128)(2,1)S(1)}, u32[]{:S(2)}, u32[]{:S(2)}) %collective-permute-start.13) | collective-permute-done | bytes 147488 | tf_op jit(solution)/shard_map/ppermute | solution.py:295
  31.5 2.5 %collective-permute-start.15 = (bf16[96,768]{1,0:T(8,128)(2,1)S(1)}, bf16[96,768]{1,0:T(8,128)(2,1)S(1)}, u32[]{:S(2)}, u32[]{:S(2)}) collective-permute-start(bf16[96,768]{1,0:T(8,128)(2,1)S(1)} %copy-done.38), channel_id=1, source_target_pairs={{0,12},{1,13},{2,14},{3,15},{4,8},{5,9},{6,10},{7,11},{8,4},{9,5},... | collective-permute-start | bytes 442376 | tf_op jit(solution)/shard_map/ppermute | solution.py:295
  34.0 2.5 %collective-permute-start.16 = (bf16[96,768]{1,0:T(8,128)(2,1)S(1)}, bf16[96,768]{1,0:T(8,128)(2,1)S(1)}, u32[]{:S(2)}, u32[]{:S(2)}) collective-permute-start(bf16[96,768]{1,0:T(8,128)(2,1)S(1)} %copy-done.37), channel_id=1, source_target_pairs={{0,13},{1,12},{2,15},{3,14},{4,9},{5,8},{6,11},{7,10},{8,5},{9,4},... | collective-permute-start | bytes 442376 | tf_op jit(solution)/shard_map/ppermute | solution.py:295
  37.1 3.0 %collective-permute-start.18 = (bf16[96,768]{1,0:T(8,128)(2,1)S(1)}, bf16[96,768]{1,0:T(8,128)(2,1)S(1)}, u32[]{:S(2)}, u32[]{:S(2)}) collective-permute-start(bf16[96,768]{1,0:T(8,128)(2,1)S(1)} %copy-done.35), channel_id=1, source_target_pairs={{0,15},{1,14},{2,13},{3,12},{4,11},{5,10},{6,9},{7,8},{8,7},{9,6},... | collective-permute-start | bytes 442376 | tf_op jit(solution)/shard_map/ppermute | solution.py:295
  40.2 3.6 %collective-permute-start.20 = (bf16[96,768]{1,0:T(8,128)(2,1)S(1)}, bf16[96,768]{1,0:T(8,128)(2,1)S(1)}, u32[]{:S(2)}, u32[]{:S(2)}) collective-permute-start(bf16[96,768]{1,0:T(8,128)(2,1)S(1)} %copy-done.33), channel_id=1, source_target_pairs={{0,9},{1,8},{2,11},{3,10},{4,1},{5,0},{6,3},{7,2},{8,13},{9,12},{1... | collective-permute-start | bytes 442376 | tf_op jit(solution)/shard_map/ppermute | solution.py:295
  43.9 15.5 %collective-permute-start.21 = (bf16[96,768]{1,0:T(8,128)(2,1)S(1)}, bf16[96,768]{1,0:T(8,128)(2,1)S(1)}, u32[]{:S(2)}, u32[]{:S(2)}) collective-permute-start(bf16[96,768]{1,0:T(8,128)(2,1)S(1)} %copy-done.32), channel_id=1, source_target_pairs={{0,10},{1,11},{2,8},{3,9},{4,2},{5,3},{6,0},{7,1},{8,14},{9,15},{1... | collective-permute-start | bytes 442376 | tf_op jit(solution)/shard_map/ppermute | solution.py:295
  59.4 2.1 %collective-permute-start.22 = (bf16[96,768]{1,0:T(8,128)(2,1)S(1)}, bf16[96,768]{1,0:T(8,128)(2,1)S(1)}, u32[]{:S(2)}, u32[]{:S(2)}) collective-permute-start(bf16[96,768]{1,0:T(8,128)(2,1)S(1)} %copy-done.31), channel_id=1, source_target_pairs={{0,11},{1,10},{2,9},{3,8},{4,3},{5,2},{6,1},{7,0},{8,15},{9,14},{1... | collective-permute-start | bytes 442376 | tf_op jit(solution)/shard_map/ppermute | solution.py:295
  62.2 7.9 %first.1 = (bf16[768,384]{1,0:T(8,128)(2,1)}, f32[768,128]{1,0:T(8,128)}, f32[768,384]{1,0:T(8,128)}) custom-call(s32[1,27]{1,0:T(1,128)} %refs_0_.3, s32[1,27]{1,0:T(1,128)} %copy-done.30, bf16[96,384]{1,0:T(8,128)(2,1)} %get-tuple-element.40.refs_2_, bf16[96,384]{1,0:T(8,128)(2,1)} %copy-done.15, bf16[96,384]{1,0:T(8,128)(2,1)} %copy-done.16, ...), custom_call_target="tpu_custom_call" | custom-call | tf_op jit(solution)/shard_map/first/pallas_call | solution.py:242
  70.9 8.5 %last.1 = (bf16[96,384]{1,0:T(8,128)(2,1)}, bf16[96,384]{1,0:T(8,128)(2,1)}, bf16[96,384]{1,0:T(8,128)(2,1)}, bf16[96,384]{1,0:T(8,128)(2,1)}, bf16[96,384]{1,0:...) custom-call(s32[1,27]{1,0:T(1,128)} %refs_0_.3, s32[1,27]{1,0:T(1,128)} %copy-done.30, ...), custom_call_target="tpu_custom_call" | custom-call | tf_op jit(solution)/shard_map/last/pallas_call | solution.py:261
  79.5 8.8 %collective-permute-start.23 = (bf16[96,384]{1,0:T(8,128)(2,1)}, bf16[96,384]{1,0:T(8,128)(2,1)S(1)}, u32[]{:S(2)}, u32[]{:S(2)}) collective-permute-start(bf16[96,384]{1,0:T(8,128)(2,1)} %get-tuple-element.68), channel_id=1, source_target_pairs={{0,1},{1,0},{2,3},{3,2},{4,5},{5,4},{6,7},{7,6},{8,9},{9,8},{10,11... | collective-permute-start | bytes 221192 | tf_op jit(solution)/shard_map/ppermute | solution.py:295
  89.7 2.1 %collective-permute-start.27 = (bf16[96,384]{1,0:T(8,128)(2,1)}, bf16[96,384]{1,0:T(8,128)(2,1)S(1)}, u32[]{:S(2)}, u32[]{:S(2)}) collective-permute-start(bf16[96,384]{1,0:T(8,128)(2,1)} %get-tuple-element.72), channel_id=1, source_target_pairs={{0,5},{1,4},{2,7},{3,6},{4,1},{5,0},{6,3},{7,2},{8,13},{9,12},{10,... | collective-permute-start | bytes 221192 | tf_op jit(solution)/shard_map/ppermute | solution.py:295
  91.9 1.7 %collective-permute-done.24.refs_2_ = bf16[96,384]{1,0:T(8,128)(2,1)S(1)} collective-permute-done((bf16[96,384]{1,0:T(8,128)(2,1)}, bf16[96,384]{1,0:T(8,128)(2,1)S(1)}, u32[]{:S(2)}, u32[]{:S(2)}) %collective-permute-start.24) | collective-permute-done | bytes 73760 | tf_op jit(solution)/shard_map/ppermute | solution.py:295
  97.4 1.6 %collective-permute-done.29.refs_7_ = bf16[96,384]{1,0:T(8,128)(2,1)S(1)} collective-permute-done((bf16[96,384]{1,0:T(8,128)(2,1)}, bf16[96,384]{1,0:T(8,128)(2,1)S(1)}, u32[]{:S(2)}, u32[]{:S(2)}) %collective-permute-start.29) | collective-permute-done | bytes 73760 | tf_op jit(solution)/shard_map/ppermute | solution.py:295
  99.6 2.0 %join.1 = bf16[96,3072]{1,0:T(8,128)(2,1)} custom-call(bf16[96,384]{1,0:T(8,128)(2,1)} %get-tuple-element.67.refs_0_, bf16[96,384]{1,0:T(8,128)(2,1)} %copy-done.22, bf16[96,384]{1,0:T(8,128)(2,1)} %copy-done.23, bf16[96,384]{1,0:T(8,128)(2,1)} %copy-done.24, bf16[96,384]{1,0:T(8,128)(2,1)} %copy-done.25, bf16[96,384]{1,0:T(8,128)(2,1)} %copy-done.26, ...), custom_call_target="tpu_custom_call" | custom-call | tf_op jit(solution)/shard_map/join/pallas_call | solution.py:282
  (119 shorter events, 14.2 us)
Async XLA Ops:
  3.2 7.7 %collective-permute-start.1 = (bf16[96,384]{1,0:T(8,128)(2,1)}, bf16[96,384]{1,0:T(8,128)(2,1)S(1)}, u32[]{:S(2)}, u32[]{:S(2)}) collective-permute-start(bf16[96,384]{1,0:T(8,128)(2,1)} %get-tuple-element.41), channel_id=1, source_target_pairs={{0,1},{1,0},{2,3},{3,2},{4,5},{5,4},{6,7},{7,6},{8,9},{9,8},{10,11... | collective-permute-start | bytes 221192 | tf_op jit(solution)/shard_map/ppermute | solution.py:295
  3.7 9.0 %collective-permute-start.2 = (bf16[96,384]{1,0:T(8,128)(2,1)}, bf16[96,384]{1,0:T(8,128)(2,1)S(1)}, u32[]{:S(2)}, u32[]{:S(2)}) collective-permute-start(bf16[96,384]{1,0:T(8,128)(2,1)} %get-tuple-element.42), channel_id=1, source_target_pairs={{0,2},{1,3},{2,0},{3,1},{4,6},{5,7},{6,4},{7,5},{8,10},{9,11},{10,... | collective-permute-start | bytes 221192 | tf_op jit(solution)/shard_map/ppermute | solution.py:295
  6.3 10.0 %collective-permute-start.3 = (bf16[96,384]{1,0:T(8,128)(2,1)}, bf16[96,384]{1,0:T(8,128)(2,1)S(1)}, u32[]{:S(2)}, u32[]{:S(2)}) collective-permute-start(bf16[96,384]{1,0:T(8,128)(2,1)} %get-tuple-element.43), channel_id=1, source_target_pairs={{0,3},{1,2},{2,1},{3,0},{4,7},{5,6},{6,5},{7,4},{8,11},{9,10},{10,... | collective-permute-start | bytes 221192 | tf_op jit(solution)/shard_map/ppermute | solution.py:295
  8.2 8.6 %collective-permute-start.4 = (bf16[96,384]{1,0:T(8,128)(2,1)}, bf16[96,384]{1,0:T(8,128)(2,1)S(1)}, u32[]{:S(2)}, u32[]{:S(2)}) collective-permute-start(bf16[96,384]{1,0:T(8,128)(2,1)} %get-tuple-element.44), channel_id=1, source_target_pairs={{0,4},{1,5},{2,6},{3,7},{4,0},{5,1},{6,2},{7,3},{8,12},{9,13},{10,... | collective-permute-start | bytes 221192 | tf_op jit(solution)/shard_map/ppermute | solution.py:295
  9.9 9.1 %collective-permute-start.5 = (bf16[96,384]{1,0:T(8,128)(2,1)}, bf16[96,384]{1,0:T(8,128)(2,1)S(1)}, u32[]{:S(2)}, u32[]{:S(2)}) collective-permute-start(bf16[96,384]{1,0:T(8,128)(2,1)} %get-tuple-element.45), channel_id=1, source_target_pairs={{0,5},{1,4},{2,7},{3,6},{4,1},{5,0},{6,3},{7,2},{8,13},{9,12},{10,... | collective-permute-start | bytes 221192 | tf_op jit(solution)/shard_map/ppermute | solution.py:295
  10.9 10.2 %collective-permute-start.6 = (bf16[96,384]{1,0:T(8,128)(2,1)}, bf16[96,384]{1,0:T(8,128)(2,1)S(1)}, u32[]{:S(2)}, u32[]{:S(2)}) collective-permute-start(bf16[96,384]{1,0:T(8,128)(2,1)} %get-tuple-element.46), channel_id=1, source_target_pairs={{0,6},{1,7},{2,4},{3,5},{4,2},{5,3},{6,0},{7,1},{8,14},{9,15},{10,... | collective-permute-start | bytes 221192 | tf_op jit(solution)/shard_map/ppermute | solution.py:295
  12.8 8.9 %collective-permute-start.7 = (bf16[96,384]{1,0:T(8,128)(2,1)}, bf16[96,384]{1,0:T(8,128)(2,1)S(1)}, u32[]{:S(2)}, u32[]{:S(2)}) collective-permute-start(bf16[96,384]{1,0:T(8,128)(2,1)} %get-tuple-element.47), channel_id=1, source_target_pairs={{0,7},{1,6},{2,5},{3,4},{4,3},{5,2},{6,1},{7,0},{8,15},{9,14},{10,... | collective-permute-start | bytes 221192 | tf_op jit(solution)/shard_map/ppermute | solution.py:295
  16.3 7.9 %collective-permute-start.11 = (bf16[96,768]{1,0:T(8,128)(2,1)}, bf16[96,768]{1,0:T(8,128)(2,1)S(1)}, u32[]{:S(2)}, u32[]{:S(2)}) collective-permute-start(bf16[96,768]{1,0:T(8,128)(2,1)} %get-tuple-element.52), channel_id=1, source_target_pairs={{0,4},{1,5},{2,6},{3,7},{4,12},{5,13},{6,14},{7,15},{8,0},{9,1},{1... | collective-permute-start | bytes 442376 | tf_op jit(solution)/shard_map/ppermute | solution.py:295
  16.7 8.9 %collective-permute-start.12 = (bf16[96,768]{1,0:T(8,128)(2,1)}, bf16[96,768]{1,0:T(8,128)(2,1)S(1)}, u32[]{:S(2)}, u32[]{:S(2)}) collective-permute-start(bf16[96,768]{1,0:T(8,128)(2,1)} %get-tuple-element.53), channel_id=1, source_target_pairs={{0,5},{1,4},{2,7},{3,6},{4,13},{5,12},{6,15},{7,14},{8,1},{9,0},{1... | collective-permute-start | bytes 442376 | tf_op jit(solution)/shard_map/ppermute | solution.py:295
  19.0 12.5 %collective-permute-start.13 = (bf16[96,768]{1,0:T(8,128)(2,1)}, bf16[96,768]{1,0:T(8,128)(2,1)S(1)}, u32[]{:S(2)}, u32[]{:S(2)}) collective-permute-start(bf16[96,768]{1,0:T(8,128)(2,1)} %get-tuple-element.54), channel_id=1, source_target_pairs={{0,6},{1,7},{2,4},{3,5},{4,14},{5,15},{6,12},{7,13},{8,2},{9,3},{1... | collective-permute-start | bytes 442376 | tf_op jit(solution)/shard_map/ppermute | solution.py:295
  21.0 13.0 %collective-permute-start.14 = (bf16[96,768]{1,0:T(8,128)(2,1)}, bf16[96,768]{1,0:T(8,128)(2,1)S(1)}, u32[]{:S(2)}, u32[]{:S(2)}) collective-permute-start(bf16[96,768]{1,0:T(8,128)(2,1)} %get-tuple-element.55), channel_id=1, source_target_pairs={{0,7},{1,6},{2,5},{3,4},{4,15},{5,14},{6,13},{7,12},{8,3},{9,2},{1... | collective-permute-start | bytes 442376 | tf_op jit(solution)/shard_map/ppermute | solution.py:295
  21.7 14.8 %collective-permute-start.8 = (bf16[96,768]{1,0:T(8,128)(2,1)}, bf16[96,768]{1,0:T(8,128)(2,1)S(1)}, u32[]{:S(2)}, u32[]{:S(2)}) collective-permute-start(bf16[96,768]{1,0:T(8,128)(2,1)} %get-tuple-element.49), channel_id=1, source_target_pairs={{0,1},{1,0},{2,3},{3,2},{4,5},{5,4},{6,7},{7,6},{8,9},{9,8},{10,11... | collective-permute-start | bytes 442376 | tf_op jit(solution)/shard_map/ppermute | solution.py:295
  24.2 13.0 %collective-permute-start.9 = (bf16[96,768]{1,0:T(8,128)(2,1)}, bf16[96,768]{1,0:T(8,128)(2,1)S(1)}, u32[]{:S(2)}, u32[]{:S(2)}) collective-permute-start(bf16[96,768]{1,0:T(8,128)(2,1)} %get-tuple-element.50), channel_id=1, source_target_pairs={{0,2},{1,3},{2,0},{3,1},{4,6},{5,7},{6,4},{7,5},{8,10},{9,11},{10,... | collective-permute-start | bytes 442376 | tf_op jit(solution)/shard_map/ppermute | solution.py:295
  25.7 14.5 %collective-permute-start.10 = (bf16[96,768]{1,0:T(8,128)(2,1)}, bf16[96,768]{1,0:T(8,128)(2,1)S(1)}, u32[]{:S(2)}, u32[]{:S(2)}) collective-permute-start(bf16[96,768]{1,0:T(8,128)(2,1)} %get-tuple-element.51), channel_id=1, source_target_pairs={{0,3},{1,2},{2,1},{3,0},{4,7},{5,6},{6,5},{7,4},{8,11},{9,10},{10,... | collective-permute-start | bytes 442376 | tf_op jit(solution)/shard_map/ppermute | solution.py:295
  31.5 8.7 %collective-permute-start.15 = (bf16[96,768]{1,0:T(8,128)(2,1)S(1)}, bf16[96,768]{1,0:T(8,128)(2,1)S(1)}, u32[]{:S(2)}, u32[]{:S(2)}) collective-permute-start(bf16[96,768]{1,0:T(8,128)(2,1)S(1)} %copy-done.38), channel_id=1, source_target_pairs={{0,12},{1,13},{2,14},{3,15},{4,8},{5,9},{6,10},{7,11},{8,4},{9,5},... | collective-permute-start | bytes 442376 | tf_op jit(solution)/shard_map/ppermute | solution.py:295
  34.0 9.9 %collective-permute-start.16 = (bf16[96,768]{1,0:T(8,128)(2,1)S(1)}, bf16[96,768]{1,0:T(8,128)(2,1)S(1)}, u32[]{:S(2)}, u32[]{:S(2)}) collective-permute-start(bf16[96,768]{1,0:T(8,128)(2,1)S(1)} %copy-done.37), channel_id=1, source_target_pairs={{0,13},{1,12},{2,15},{3,14},{4,9},{5,8},{6,11},{7,10},{8,5},{9,4},... | collective-permute-start | bytes 442376 | tf_op jit(solution)/shard_map/ppermute | solution.py:295
  36.5 22.9 %collective-permute-start.17 = (bf16[96,768]{1,0:T(8,128)(2,1)S(1)}, bf16[96,768]{1,0:T(8,128)(2,1)S(1)}, u32[]{:S(2)}, u32[]{:S(2)}) collective-permute-start(bf16[96,768]{1,0:T(8,128)(2,1)S(1)} %copy-done.36), channel_id=1, source_target_pairs={{0,14},{1,15},{2,12},{3,13},{4,10},{5,11},{6,8},{7,9},{8,6},{9,7},... | collective-permute-start | bytes 442376 | tf_op jit(solution)/shard_map/ppermute | solution.py:295
  37.1 24.4 %collective-permute-start.18 = (bf16[96,768]{1,0:T(8,128)(2,1)S(1)}, bf16[96,768]{1,0:T(8,128)(2,1)S(1)}, u32[]{:S(2)}, u32[]{:S(2)}) collective-permute-start(bf16[96,768]{1,0:T(8,128)(2,1)S(1)} %copy-done.35), channel_id=1, source_target_pairs={{0,15},{1,14},{2,13},{3,12},{4,11},{5,10},{6,9},{7,8},{8,7},{9,6},... | collective-permute-start | bytes 442376 | tf_op jit(solution)/shard_map/ppermute | solution.py:295
  40.1 30.0 %collective-permute-start.19 = (bf16[96,768]{1,0:T(8,128)(2,1)S(1)}, bf16[96,768]{1,0:T(8,128)(2,1)S(1)}, u32[]{:S(2)}, u32[]{:S(2)}) collective-permute-start(bf16[96,768]{1,0:T(8,128)(2,1)S(1)} %copy-done.34), channel_id=1, source_target_pairs={{0,8},{1,9},{2,10},{3,11},{4,0},{5,1},{6,2},{7,3},{8,12},{9,13},{1... | collective-permute-start | bytes 442376 | tf_op jit(solution)/shard_map/ppermute | solution.py:295
  40.2 29.9 %collective-permute-start.20 = (bf16[96,768]{1,0:T(8,128)(2,1)S(1)}, bf16[96,768]{1,0:T(8,128)(2,1)S(1)}, u32[]{:S(2)}, u32[]{:S(2)}) collective-permute-start(bf16[96,768]{1,0:T(8,128)(2,1)S(1)} %copy-done.33), channel_id=1, source_target_pairs={{0,9},{1,8},{2,11},{3,10},{4,1},{5,0},{6,3},{7,2},{8,13},{9,12},{1... | collective-permute-start | bytes 442376 | tf_op jit(solution)/shard_map/ppermute | solution.py:295
  43.9 26.3 %collective-permute-start.21 = (bf16[96,768]{1,0:T(8,128)(2,1)S(1)}, bf16[96,768]{1,0:T(8,128)(2,1)S(1)}, u32[]{:S(2)}, u32[]{:S(2)}) collective-permute-start(bf16[96,768]{1,0:T(8,128)(2,1)S(1)} %copy-done.32), channel_id=1, source_target_pairs={{0,10},{1,11},{2,8},{3,9},{4,2},{5,3},{6,0},{7,1},{8,14},{9,15},{1... | collective-permute-start | bytes 442376 | tf_op jit(solution)/shard_map/ppermute | solution.py:295
  59.4 10.7 %collective-permute-start.22 = (bf16[96,768]{1,0:T(8,128)(2,1)S(1)}, bf16[96,768]{1,0:T(8,128)(2,1)S(1)}, u32[]{:S(2)}, u32[]{:S(2)}) collective-permute-start(bf16[96,768]{1,0:T(8,128)(2,1)S(1)} %copy-done.31), channel_id=1, source_target_pairs={{0,11},{1,10},{2,9},{3,8},{4,3},{5,2},{6,1},{7,0},{8,15},{9,14},{1... | collective-permute-start | bytes 442376 | tf_op jit(solution)/shard_map/ppermute | solution.py:295
  79.5 12.3 %collective-permute-start.23 = (bf16[96,384]{1,0:T(8,128)(2,1)}, bf16[96,384]{1,0:T(8,128)(2,1)S(1)}, u32[]{:S(2)}, u32[]{:S(2)}) collective-permute-start(bf16[96,384]{1,0:T(8,128)(2,1)} %get-tuple-element.68), channel_id=1, source_target_pairs={{0,1},{1,0},{2,3},{3,2},{4,5},{5,4},{6,7},{7,6},{8,9},{9,8},{10,11... | collective-permute-start | bytes 221192 | tf_op jit(solution)/shard_map/ppermute | solution.py:295
  89.7 6.4 %collective-permute-start.27 = (bf16[96,384]{1,0:T(8,128)(2,1)}, bf16[96,384]{1,0:T(8,128)(2,1)S(1)}, u32[]{:S(2)}, u32[]{:S(2)}) collective-permute-start(bf16[96,384]{1,0:T(8,128)(2,1)} %get-tuple-element.72), channel_id=1, source_target_pairs={{0,5},{1,4},{2,7},{3,6},{4,1},{5,0},{6,3},{7,2},{8,13},{9,12},{10,... | collective-permute-start | bytes 221192 | tf_op jit(solution)/shard_map/ppermute | solution.py:295
  (45 other events, 973.3 us)

commit v2 on v1

--- a/solution.py
+++ b/solution.py
@@ -88,6 +88,7 @@
 ACROSS = (3, 2, 1, 0)
 MASKED = -1e30
 FACTOR = math.log2(math.e) / math.sqrt(HDIM)
+KERNEL_VMEM = 28 << 20
 
 
 def flipped(index, bits, size):
@@ -174,62 +175,74 @@
     return z, 2 * (1 - mate) + pair, 3 - z, 2 * mate + 1 - pair
 
 
-def softmax_part(q, k, v, bias):
+def fill(kbuf, vbuf, pieces, width):
+    rows = pieces[0].shape[0]
+    ones = jnp.ones((rows, HDIM), jnp.bfloat16)
+    for s, piece in enumerate(pieces):
+        at = slice(s * rows, (s + 1) * rows)
+        kbuf[at, :] = piece[:, :width]
+        for h in range(width // HDIM):
+            vbuf[at, 2 * h * HDIM : (2 * h + 1) * HDIM] = piece[
+                :, width + h * HDIM : width + (h + 1) * HDIM
+            ]
+            vbuf[at, (2 * h + 1) * HDIM : (2 * h + 2) * HDIM] = ones
+
+
+def scores_of(q, k, bias):
     scores = lax.dot_general(q, k, (((1,), (1,)), ((), ())), preferred_element_type=jnp.float32)
-    scores = scores + bias
-    peak = jnp.max(scores, axis=1, keepdims=True)
-    weight = jnp.exp2((scores - peak) * FACTOR)
-    total = jnp.sum(weight, axis=1, keepdims=True)
-    mixed = jnp.dot(weight.astype(jnp.bfloat16), v, preferred_element_type=jnp.float32)
-    return peak, total, mixed
+    return scores + bias
+
+
+def mixed_of(scores, peak, v):
+    weight = jnp.exp2((scores - peak) * FACTOR).astype(jnp.bfloat16)
+    return jnp.dot(weight, v, preferred_element_type=jnp.float32)
 
 
 def first_kernel(heads, width, *refs):
     masks, refs = refs[:2], refs[2:]
     queries, refs = refs[: 2 * heads], refs[2 * heads :]
-    pieces, refs = refs[: 3 * heads], refs[3 * heads :]
-    q_out, stat_out, mixed_out, kbuf, vbuf = refs
+    pieces, refs = refs[: 2 * heads], refs[2 * heads :]
+    q_out, peak_out, mixed_out, kbuf, vbuf = refs
     rows = queries[0].shape[0]
     tile = heads * rows
     for s, piece in enumerate(queries):
         q_out[s * rows : (s + 1) * rows, :] = piece[...]
-    for s, piece in enumerate(pieces):
-        kbuf[s * rows : (s + 1) * rows, :] = piece[:, :width]
-        vbuf[s * rows : (s + 1) * rows, :] = piece[:, width:]
+    fill(kbuf, vbuf, pieces, width)
     for own in range(2):
-        bias = tile_bias(masks, own, key_blocks()[:3], tile)
+        bias = tile_bias(masks, own, key_blocks()[:2], tile)
         at = slice(own * tile, (own + 1) * tile)
         for h in range(width // HDIM):
             cols = slice(h * HDIM, (h + 1) * HDIM)
-            peak, total, mixed = softmax_part(q_out[at, cols], kbuf[:, cols], vbuf[:, cols], bias)
-            stat_out[at, 2 * h : 2 * h + 1] = peak
-            stat_out[at, 2 * h + 1 : 2 * h + 2] = total
-            mixed_out[at, cols] = mixed
+            both = slice(2 * h * HDIM, (2 * h + 2) * HDIM)
+            scores = scores_of(q_out[at, cols], kbuf[:, cols], bias)
+            peak = jnp.max(scores, axis=1, keepdims=True)
+            peak_out[at, cols] = jnp.broadcast_to(peak, (tile, HDIM))
+            mixed_out[at, both] = mixed_of(scores, peak, vbuf[:, both])
 
 
 def last_kernel(heads, width, *refs):
     masks, refs = refs[:2], refs[2:]
-    q_ref, stat_ref, mixed_ref, refs = refs[0], refs[1], refs[2], refs[3:]
-    pieces, refs = refs[:heads], refs[heads:]
+    q_ref, peak_ref, mixed_ref, refs = refs[0], refs[1], refs[2], refs[3:]
+    pieces, refs = refs[: 2 * heads], refs[2 * heads :]
     outs, kbuf, vbuf = refs[: 2 * heads], refs[2 * heads], refs[2 * heads + 1]
     rows = pieces[0].shape[0]
     tile = heads * rows
-    for s, piece in enumerate(pieces):
-        kbuf[s * rows : (s + 1) * rows, :] = piece[:, :width]
-        vbuf[s * rows : (s + 1) * rows, :] = piece[:, width:]
-    for own in range(2):
-        bias = tile_bias(masks, own, key_blocks()[3:], tile)
+    fill(kbuf, vbuf, pieces, width)
+    for own in (1, 0):
+        bias = tile_bias(masks, own, key_blocks()[2:], tile)
         at = slice(own * tile, (own + 1) * tile)
         for h in range(width // HDIM):
             cols = slice(h * HDIM, (h + 1) * HDIM)
-            peak, total, mixed = softmax_part(q_ref[at, cols], kbuf[:, cols], vbuf[:, cols], bias)
-            old_peak = stat_ref[at, 2 * h : 2 * h + 1]
-            old_total = stat_ref[at, 2 * h + 1 : 2 * h + 2]
-            top = jnp.maximum(peak, old_peak)
-            new_share = jnp.exp2((peak - top) * FACTOR)
-            old_share = jnp.exp2((old_peak - top) * FACTOR)
-            total = total * new_share + old_total * old_share
-            mixed = mixed * new_share + mixed_ref[at, cols] * old_share
+            both = slice(2 * h * HDIM, (2 * h + 2) * HDIM)
+            scores = scores_of(q_ref[at, cols], kbuf[:, cols], bias)
+            old_peak = peak_ref[at, cols]
+            peak = jnp.broadcast_to(jnp.max(scores, axis=1, keepdims=True), (tile, HDIM))
+            peak = jnp.maximum(peak, old_peak)
+            share = jnp.exp2((old_peak - peak) * FACTOR)
+            wide = jnp.concatenate([peak] * (2 * tile // HDIM), axis=1)
+            mixed = mixed_of(scores, wide, vbuf[:, both])
+            total = mixed[:, HDIM:] + mixed_ref[at, both][:, HDIM:] * share
+            mixed = mixed[:, :HDIM] + mixed_ref[at, both][:, :HDIM] * share
             result = (mixed / total).astype(jnp.bfloat16)
             for n in range(heads):
                 outs[own * heads + n][:, cols] = result[n * rows : (n + 1) * rows]
@@ -243,13 +256,17 @@
         functools.partial(first_kernel, heads, width),
         out_shape=[
             jax.ShapeDtypeStruct((2 * tile, width), jnp.bfloat16),
-            jax.ShapeDtypeStruct((2 * tile, 128), jnp.float32),
             jax.ShapeDtypeStruct((2 * tile, width), jnp.float32),
+            jax.ShapeDtypeStruct((2 * tile, 2 * width), jnp.float32),
         ],
         in_specs=[pl.BlockSpec(memory_space=pltpu.SMEM)] * 2
         + [vmem] * (len(queries) + len(pieces)),
         out_specs=[vmem] * 3,
-        scratch_shapes=[pltpu.VMEM((3 * tile, width), jnp.bfloat16)] * 2,
+        scratch_shapes=[
+            pltpu.VMEM((2 * tile, width), jnp.bfloat16),
+            pltpu.VMEM((2 * tile, 2 * width), jnp.bfloat16),
+        ],
+        compiler_params=pltpu.CompilerParams(vmem_limit_bytes=KERNEL_VMEM),
         name="first",
     )(*masks, *queries, *pieces)
 
@@ -263,27 +280,33 @@
         out_shape=[jax.ShapeDtypeStruct((rows, width), jnp.bfloat16)] * (2 * heads),
         in_specs=[pl.BlockSpec(memory_space=pltpu.SMEM)] * 2 + [vmem] * (3 + len(pieces)),
         out_specs=[vmem] * (2 * heads),
-        scratch_shapes=[pltpu.VMEM((tile, width), jnp.bfloat16)] * 2,
+        scratch_shapes=[
+            pltpu.VMEM((2 * tile, width), jnp.bfloat16),
+            pltpu.VMEM((2 * tile, 2 * width), jnp.bfloat16),
+        ],
+        compiler_params=pltpu.CompilerParams(vmem_limit_bytes=KERNEL_VMEM),
         name="last",
     )(*masks, *carried, *pieces)
 
 
 def join_kernel(heads, width, *refs):
-    pieces, out = refs[:-1], refs[-1]
+    pieces, out, sem = refs[:-2], refs[-2], refs[-1]
     own = lax.axis_index("mate")
+    copies = []
     for s, piece in enumerate(pieces):
         mate = 1 - own if s >= heads else own
-        out[:, columns_of(mate, s % heads, heads, width)] = piece[...]
+        copies.append((piece, out.at[:, columns_of(mate, s % heads, heads, width)]))
+    copy_all(copies, sem)
 
 
 def join(pieces, heads, width):
     rows = pieces[0].shape[0]
-    vmem = pl.BlockSpec(memory_space=pltpu.VMEM)
     return pl.pallas_call(
         functools.partial(join_kernel, heads, width),
         out_shape=jax.ShapeDtypeStruct((rows, 2 * heads * width), jnp.bfloat16),
-        in_specs=[vmem] * len(pieces),
-        out_specs=vmem,
+        in_specs=[pl.BlockSpec(memory_space=pltpu.VMEM)] * len(pieces),
+        out_specs=pl.BlockSpec(memory_space=pl.ANY),
+        scratch_shapes=[pltpu.SemaphoreType.DMA((len(pieces),))],
         name="join",
     )(*pieces)
 
@@ -315,8 +338,8 @@
     across = [moved(rest[heads + l], ACROSS, l, heads) for l in some]
     behind = [moved(rest[2 * heads + l], BEHIND, l, heads) for l in some]
     masks = (tile_mask, moved(tile_mask, MATE, 0, heads))
-    carried = attend_first(masks, queries, own + ahead + across, heads, width)
-    parts = attend_last(masks, carried, behind, heads, width)
+    carried = attend_first(masks, queries, own + ahead, heads, width)
+    parts = attend_last(masks, carried, across + behind, heads, width)
     order = [s for s in range(heads, 2 * heads)] + list(some[1:])
     back = {0: parts[0]}
     for s in order:

time: 102 us -> 93 us (0.912)
  Pallas kernels: 23.7 us -> 14 us
  local copies, waits for them, and re-layouts: 1.96 us -> 3.02 us
    pallas_call x1, Pallas kernels: 8.52 us -> 3.42 us  [attend_last(): pl.pallas_call(functools.partial(last_kernel, heads, width), out_shape=[j...]
    pallas_call x1, Pallas kernels: 7.91 us -> 3.33 us  [attend_first(): pl.pallas_call(functools.partial(first_kernel, heads, width), out_shape=[...]
    unnamed x78 -> x22, local copies, waits for them, and re-layouts: 1.96 us -> 3.02 us
  transfers between devices with their start and end apart: 30 -> 30, of which waited for: 8 -> 8; matrix products, arithmetic and copies ran while one was open for 0% -> 0% of each run, Pallas kernels for 10% -> 6%
where the time goes in v2:
time: 93 us; the launch traced here: 92.7 us
  starting transfers between devices  62.7 us (67%)
  Pallas kernels  14 us (15%)
  waiting for transfers between devices  12.9 us (14%)
  local copies, waits for them, and re-layouts  3.02 us (3%)
    ppermute x30, starting transfers between devices, moved(): return lax.ppermute(block, AXES, route)  62.7 us
    ppermute x30, waiting for transfers between devices, moved(): return lax.ppermute(block, AXES, route)  12.9 us
    pallas_call x2, Pallas kernels, cut_call(): pl.pallas_call(functools.partial(kernel, heads, width), out_shape=shapes,...  5.22 us
    pallas_call x1, Pallas kernels, attend_last(): pl.pallas_call(functools.partial(last_kernel, heads, width), out_shape=[j...  3.42 us
    pallas_call x1, Pallas kernels, attend_first(): pl.pallas_call(functools.partial(first_kernel, heads, width), out_shape=[...  3.33 us
    unnamed x22, local copies, waits for them, and re-layouts  3.02 us
    pallas_call x1, Pallas kernels, join(): pl.pallas_call(functools.partial(join_kernel, heads, width), out_shape=ja...  2.01 us
  transfers between devices with their start and end apart: 30, of which 8 were waited for; matrix products, arithmetic and copies ran while one was open for 0% of the time, Pallas kernels for 6%

profile of v2, /device:TPU:0, one launch (start us, length us, event | category | flops | bytes accessed | tf_op | source)
XLA Modules:
  0.0 92.7 jit_solution(4366181796768260125)
XLA Ops:
  0.0 3.1 %shard_map.46 = (bf16[96,768]{1,0:T(8,128)(2,1)}, bf16[96,768]{1,0:T(8,128)(2,1)}, bf16[96,768]{1,0:T(8,128)(2,1)}, bf16[96,768]{1,0:T(8,128)(2,1)}, bf16[96,768...) custom-call(bf16[96,3072]{1,0:T(8,128)(2,1)} %q_ref.1, ...), custom_call_target="tpu_custom_call" | custom-call | tf_op jit(solution)/shard_map/pallas_call | solution.py:145
  3.7 2.6 %collective-permute-start.2 = (bf16[96,384]{1,0:T(8,128)(2,1)}, bf16[96,384]{1,0:T(8,128)(2,1)S(1)}, u32[]{:S(2)}, u32[]{:S(2)}) collective-permute-start(bf16[96,384]{1,0:T(8,128)(2,1)} %get-tuple-element.42), channel_id=1, source_target_pairs={{0,2},{1,3},{2,0},{3,1},{4,6},{5,7},{6,4},{7,5},{8,10},{9,11},{10,... | collective-permute-start | bytes 221192 | tf_op jit(solution)/shard_map/ppermute | solution.py:318
  6.3 1.8 %collective-permute-start = (s32[1,27]{1,0:T(1,128)}, s32[1,27]{1,0:T(1,128)S(1)}, u32[]{:S(2)}, u32[]{:S(2)}) collective-permute-start(s32[1,27]{1,0:T(1,128)} %refs_0_.3), channel_id=1, source_target_pairs={{0,4},{1,5},{2,6},{3,7},{4,0},{5,1},{6,2},{7,3},{8,12},{9,13},{10,... | collective-permute-start | bytes 332 | tf_op jit(solution)/shard_map/ppermute | solution.py:318
  8.3 1.7 %collective-permute-done.refs_1_ = s32[1,27]{1,0:T(1,128)S(1)} collective-permute-done((s32[1,27]{1,0:T(1,128)}, s32[1,27]{1,0:T(1,128)S(1)}, u32[]{:S(2)}, u32[]{:S(2)}) %collective-permute-start) | collective-permute-done | bytes 140 | tf_op jit(solution)/shard_map/ppermute | solution.py:318
  10.9 1.8 %collective-permute-start.6 = (bf16[96,384]{1,0:T(8,128)(2,1)}, bf16[96,384]{1,0:T(8,128)(2,1)S(1)}, u32[]{:S(2)}, u32[]{:S(2)}) collective-permute-start(bf16[96,384]{1,0:T(8,128)(2,1)} %get-tuple-element.46), channel_id=1, source_target_pairs={{0,6},{1,7},{2,4},{3,5},{4,2},{5,3},{6,0},{7,1},{8,14},{9,15},{10,... | collective-permute-start | bytes 221192 | tf_op jit(solution)/shard_map/ppermute | solution.py:318
  14.2 2.1 %shard_map.47 = (bf16[96,768]{1,0:T(8,128)(2,1)}, bf16[96,768]{1,0:T(8,128)(2,1)}, bf16[96,768]{1,0:T(8,128)(2,1)}, bf16[96,768]{1,0:T(8,128)(2,1)}) custom-call(bf16[96,3072]{1,0:T(8,128)(2,1)} %k_ref.3, bf16[96,3072]{1,0:T(8,128)(2,1)} %v_ref.3), custom_call_target="tpu_custom_call" | custom-call | tf_op jit(solution)/shard_map/pallas_call | solution.py:145
  16.7 2.2 %collective-permute-start.12 = (bf16[96,768]{1,0:T(8,128)(2,1)}, bf16[96,768]{1,0:T(8,128)(2,1)S(1)}, u32[]{:S(2)}, u32[]{:S(2)}) collective-permute-start(bf16[96,768]{1,0:T(8,128)(2,1)} %get-tuple-element.53), channel_id=1, source_target_pairs={{0,5},{1,4},{2,7},{3,6},{4,13},{5,12},{6,15},{7,14},{8,1},{9,0},{1... | collective-permute-start | bytes 442376 | tf_op jit(solution)/shard_map/ppermute | solution.py:318
  19.0 2.1 %collective-permute-start.13 = (bf16[96,768]{1,0:T(8,128)(2,1)}, bf16[96,768]{1,0:T(8,128)(2,1)S(1)}, u32[]{:S(2)}, u32[]{:S(2)}) collective-permute-start(bf16[96,768]{1,0:T(8,128)(2,1)} %get-tuple-element.54), channel_id=1, source_target_pairs={{0,6},{1,7},{2,4},{3,5},{4,14},{5,15},{6,12},{7,13},{8,2},{9,3},{1... | collective-permute-start | bytes 442376 | tf_op jit(solution)/shard_map/ppermute | solution.py:318
  22.1 2.1 %collective-permute-done.11.refs_14_ = bf16[96,768]{1,0:T(8,128)(2,1)S(1)} collective-permute-done((bf16[96,768]{1,0:T(8,128)(2,1)}, bf16[96,768]{1,0:T(8,128)(2,1)S(1)}, u32[]{:S(2)}, u32[]{:S(2)}) %collective-permute-start.11) | collective-permute-done | bytes 147488 | tf_op jit(solution)/shard_map/ppermute | solution.py:318
  24.2 1.5 %collective-permute-start.9 = (bf16[96,768]{1,0:T(8,128)(2,1)}, bf16[96,768]{1,0:T(8,128)(2,1)S(1)}, u32[]{:S(2)}, u32[]{:S(2)}) collective-permute-start(bf16[96,768]{1,0:T(8,128)(2,1)} %get-tuple-element.50), channel_id=1, source_target_pairs={{0,2},{1,3},{2,0},{3,1},{4,6},{5,7},{6,4},{7,5},{8,10},{9,11},{10,... | collective-permute-start | bytes 442376 | tf_op jit(solution)/shard_map/ppermute | solution.py:318
  25.7 2.9 %collective-permute-start.10 = (bf16[96,768]{1,0:T(8,128)(2,1)}, bf16[96,768]{1,0:T(8,128)(2,1)S(1)}, u32[]{:S(2)}, u32[]{:S(2)}) collective-permute-start(bf16[96,768]{1,0:T(8,128)(2,1)} %get-tuple-element.51), channel_id=1, source_target_pairs={{0,3},{1,2},{2,1},{3,0},{4,7},{5,6},{6,5},{7,4},{8,11},{9,10},{10,... | collective-permute-start | bytes 442376 | tf_op jit(solution)/shard_map/ppermute | solution.py:318
  28.6 3.0 %collective-permute-done.13.refs_16_ = bf16[96,768]{1,0:T(8,128)(2,1)S(1)} collective-permute-done((bf16[96,768]{1,0:T(8,128)(2,1)}, bf16[96,768]{1,0:T(8,128)(2,1)S(1)}, u32[]{:S(2)}, u32[]{:S(2)}) %collective-permute-start.13) | collective-permute-done | bytes 147488 | tf_op jit(solution)/shard_map/ppermute | solution.py:318
  31.5 2.5 %collective-permute-start.15 = (bf16[96,768]{1,0:T(8,128)(2,1)}, bf16[96,768]{1,0:T(8,128)(2,1)S(1)}, u32[]{:S(2)}, u32[]{:S(2)}) collective-permute-start(bf16[96,768]{1,0:T(8,128)(2,1)} %get-tuple-element.59), channel_id=1, source_target_pairs={{0,12},{1,13},{2,14},{3,15},{4,8},{5,9},{6,10},{7,11},{8,4},{9,5},... | collective-permute-start | bytes 442376 | tf_op jit(solution)/shard_map/ppermute | solution.py:318
  34.0 2.5 %collective-permute-start.16 = (bf16[96,768]{1,0:T(8,128)(2,1)}, bf16[96,768]{1,0:T(8,128)(2,1)S(1)}, u32[]{:S(2)}, u32[]{:S(2)}) collective-permute-start(bf16[96,768]{1,0:T(8,128)(2,1)} %get-tuple-element.60), channel_id=1, source_target_pairs={{0,13},{1,12},{2,15},{3,14},{4,9},{5,8},{6,11},{7,10},{8,5},{9,4},... | collective-permute-start | bytes 442376 | tf_op jit(solution)/shard_map/ppermute | solution.py:318
  36.9 3.0 %collective-permute-start.18 = (bf16[96,768]{1,0:T(8,128)(2,1)}, bf16[96,768]{1,0:T(8,128)(2,1)S(1)}, u32[]{:S(2)}, u32[]{:S(2)}) collective-permute-start(bf16[96,768]{1,0:T(8,128)(2,1)} %get-tuple-element.62), channel_id=1, source_target_pairs={{0,15},{1,14},{2,13},{3,12},{4,11},{5,10},{6,9},{7,8},{8,7},{9,6},... | collective-permute-start | bytes 442376 | tf_op jit(solution)/shard_map/ppermute | solution.py:318
  39.9 3.6 %collective-permute-start.20 = (bf16[96,768]{1,0:T(8,128)(2,1)}, bf16[96,768]{1,0:T(8,128)(2,1)S(1)}, u32[]{:S(2)}, u32[]{:S(2)}) collective-permute-start(bf16[96,768]{1,0:T(8,128)(2,1)} %get-tuple-element.64), channel_id=1, source_target_pairs={{0,9},{1,8},{2,11},{3,10},{4,1},{5,0},{6,3},{7,2},{8,13},{9,12},{1... | collective-permute-start | bytes 442376 | tf_op jit(solution)/shard_map/ppermute | solution.py:318
  43.4 15.9 %collective-permute-start.21 = (bf16[96,768]{1,0:T(8,128)(2,1)}, bf16[96,768]{1,0:T(8,128)(2,1)S(1)}, u32[]{:S(2)}, u32[]{:S(2)}) collective-permute-start(bf16[96,768]{1,0:T(8,128)(2,1)} %get-tuple-element.65), channel_id=1, source_target_pairs={{0,10},{1,11},{2,8},{3,9},{4,2},{5,3},{6,0},{7,1},{8,14},{9,15},{1... | collective-permute-start | bytes 442376 | tf_op jit(solution)/shard_map/ppermute | solution.py:318
  59.4 2.0 %collective-permute-start.22 = (bf16[96,768]{1,0:T(8,128)(2,1)}, bf16[96,768]{1,0:T(8,128)(2,1)S(1)}, u32[]{:S(2)}, u32[]{:S(2)}) collective-permute-start(bf16[96,768]{1,0:T(8,128)(2,1)} %get-tuple-element.66), channel_id=1, source_target_pairs={{0,11},{1,10},{2,9},{3,8},{4,3},{5,2},{6,1},{7,0},{8,15},{9,14},{1... | collective-permute-start | bytes 442376 | tf_op jit(solution)/shard_map/ppermute | solution.py:318
  63.1 3.3 %first.1 = (bf16[768,384]{1,0:T(8,128)(2,1)S(1)}, f32[768,384]{1,0:T(8,128)S(1)}, f32[768,768]{1,0:T(8,128)S(1)}) custom-call(s32[1,27]{1,0:T(1,128)S(1)} %copy-done.3, s32[1,27]{1,0:T(1,128)S(1)} %collective-permute-done.refs_1_, bf16[96,384]{1,0:T(8,128)(2,1)S(1)} %copy-done.1, bf16[96,384]{1,0:T(8,128)(2,1)S(1)} %collective-permute-done.1.refs_3_, ...), custom_call_target="tpu_custom_call" | custom-call | tf_op jit(solution)/shard_map/first/pallas_call | solution.py:255
  66.5 3.4 %last.1 = (bf16[96,384]{1,0:T(8,128)(2,1)S(1)}, bf16[96,384]{1,0:T(8,128)(2,1)S(1)}, bf16[96,384]{1,0:T(8,128)(2,1)S(1)}, bf16[96,384]{1,0:T(8,128)(2,1)S(1)}, b...) custom-call(s32[1,27]{1,0:T(1,128)S(1)} %copy-done.3, ...), custom_call_target="tpu_custom_call" | custom-call | tf_op jit(solution)/shard_map/last/pallas_call | solution.py:278
  70.6 9.1 %collective-permute-start.23 = (bf16[96,384]{1,0:T(8,128)(2,1)S(1)}, bf16[96,384]{1,0:T(8,128)(2,1)S(1)}, u32[]{:S(2)}, u32[]{:S(2)}) collective-permute-start(bf16[96,384]{1,0:T(8,128)(2,1)S(1)} %get-tuple-element.68), channel_id=1, source_target_pairs={{0,1},{1,0},{2,3},{3,2},{4,5},{5,4},{6,7},{7,6},{8,9},{9,8},{10,11... | collective-permute-start | bytes 221192 | tf_op jit(solution)/shard_map/ppermute | solution.py:318
  81.0 2.1 %collective-permute-start.27 = (bf16[96,384]{1,0:T(8,128)(2,1)S(1)}, bf16[96,384]{1,0:T(8,128)(2,1)S(1)}, u32[]{:S(2)}, u32[]{:S(2)}) collective-permute-start(bf16[96,384]{1,0:T(8,128)(2,1)S(1)} %get-tuple-element.72), channel_id=1, source_target_pairs={{0,5},{1,4},{2,7},{3,6},{4,1},{5,0},{6,3},{7,2},{8,13},{9,12},{10,... | collective-permute-start | bytes 221192 | tf_op jit(solution)/shard_map/ppermute | solution.py:318
  88.7 1.5 %collective-permute-done.29.refs_7_ = bf16[96,384]{1,0:T(8,128)(2,1)S(1)} collective-permute-done((bf16[96,384]{1,0:T(8,128)(2,1)S(1)}, bf16[96,384]{1,0:T(8,128)(2,1)S(1)}, u32[]{:S(2)}, u32[]{:S(2)}) %collective-permute-start.29) | collective-permute-done | bytes 73760 | tf_op jit(solution)/shard_map/ppermute | solution.py:318
  90.7 2.0 %join.1 = bf16[96,3072]{1,0:T(8,128)(2,1)} custom-call(bf16[96,384]{1,0:T(8,128)(2,1)} %copy-done.2, bf16[96,384]{1,0:T(8,128)(2,1)} %copy-done.4, bf16[96,384]{1,0:T(8,128)(2,1)} %copy-done.5, bf16[96,384]{1,0:T(8,128)(2,1)} %copy-done.6, bf16[96,384]{1,0:T(8,128)(2,1)} %copy-done.7, bf16[96,384]{1,0:T(8,128)(2,1)} %copy-done.8, bf16[96,384]{1,0:T(8,128)(2,1)} %copy-done.9, ...), custom_call_target="tpu_custom_call" | custom-call | tf_op jit(solution)/shard_map/join/pallas_call | solution.py:304
  (63 shorter events, 14.9 us)
Async XLA Ops:
  3.1 7.8 %collective-permute-start.1 = (bf16[96,384]{1,0:T(8,128)(2,1)}, bf16[96,384]{1,0:T(8,128)(2,1)S(1)}, u32[]{:S(2)}, u32[]{:S(2)}) collective-permute-start(bf16[96,384]{1,0:T(8,128)(2,1)} %get-tuple-element.41), channel_id=1, source_target_pairs={{0,1},{1,0},{2,3},{3,2},{4,5},{5,4},{6,7},{7,6},{8,9},{9,8},{10,11... | collective-permute-start | bytes 221192 | tf_op jit(solution)/shard_map/ppermute | solution.py:318
  3.7 9.1 %collective-permute-start.2 = (bf16[96,384]{1,0:T(8,128)(2,1)}, bf16[96,384]{1,0:T(8,128)(2,1)S(1)}, u32[]{:S(2)}, u32[]{:S(2)}) collective-permute-start(bf16[96,384]{1,0:T(8,128)(2,1)} %get-tuple-element.42), channel_id=1, source_target_pairs={{0,2},{1,3},{2,0},{3,1},{4,6},{5,7},{6,4},{7,5},{8,10},{9,11},{10,... | collective-permute-start | bytes 221192 | tf_op jit(solution)/shard_map/ppermute | solution.py:318
  6.2 10.1 %collective-permute-start.3 = (bf16[96,384]{1,0:T(8,128)(2,1)}, bf16[96,384]{1,0:T(8,128)(2,1)S(1)}, u32[]{:S(2)}, u32[]{:S(2)}) collective-permute-start(bf16[96,384]{1,0:T(8,128)(2,1)} %get-tuple-element.43), channel_id=1, source_target_pairs={{0,3},{1,2},{2,1},{3,0},{4,7},{5,6},{6,5},{7,4},{8,11},{9,10},{10,... | collective-permute-start | bytes 221192 | tf_op jit(solution)/shard_map/ppermute | solution.py:318
  8.1 8.7 %collective-permute-start.4 = (bf16[96,384]{1,0:T(8,128)(2,1)}, bf16[96,384]{1,0:T(8,128)(2,1)S(1)}, u32[]{:S(2)}, u32[]{:S(2)}) collective-permute-start(bf16[96,384]{1,0:T(8,128)(2,1)} %get-tuple-element.44), channel_id=1, source_target_pairs={{0,4},{1,5},{2,6},{3,7},{4,0},{5,1},{6,2},{7,3},{8,12},{9,13},{10,... | collective-permute-start | bytes 221192 | tf_op jit(solution)/shard_map/ppermute | solution.py:318
  10.0 9.0 %collective-permute-start.5 = (bf16[96,384]{1,0:T(8,128)(2,1)}, bf16[96,384]{1,0:T(8,128)(2,1)S(1)}, u32[]{:S(2)}, u32[]{:S(2)}) collective-permute-start(bf16[96,384]{1,0:T(8,128)(2,1)} %get-tuple-element.45), channel_id=1, source_target_pairs={{0,5},{1,4},{2,7},{3,6},{4,1},{5,0},{6,3},{7,2},{8,13},{9,12},{10,... | collective-permute-start | bytes 221192 | tf_op jit(solution)/shard_map/ppermute | solution.py:318
  10.9 10.1 %collective-permute-start.6 = (bf16[96,384]{1,0:T(8,128)(2,1)}, bf16[96,384]{1,0:T(8,128)(2,1)S(1)}, u32[]{:S(2)}, u32[]{:S(2)}) collective-permute-start(bf16[96,384]{1,0:T(8,128)(2,1)} %get-tuple-element.46), channel_id=1, source_target_pairs={{0,6},{1,7},{2,4},{3,5},{4,2},{5,3},{6,0},{7,1},{8,14},{9,15},{10,... | collective-permute-start | bytes 221192 | tf_op jit(solution)/shard_map/ppermute | solution.py:318
  12.7 9.0 %collective-permute-start.7 = (bf16[96,384]{1,0:T(8,128)(2,1)}, bf16[96,384]{1,0:T(8,128)(2,1)S(1)}, u32[]{:S(2)}, u32[]{:S(2)}) collective-permute-start(bf16[96,384]{1,0:T(8,128)(2,1)} %get-tuple-element.47), channel_id=1, source_target_pairs={{0,7},{1,6},{2,5},{3,4},{4,3},{5,2},{6,1},{7,0},{8,15},{9,14},{10,... | collective-permute-start | bytes 221192 | tf_op jit(solution)/shard_map/ppermute | solution.py:318
  16.3 7.9 %collective-permute-start.11 = (bf16[96,768]{1,0:T(8,128)(2,1)}, bf16[96,768]{1,0:T(8,128)(2,1)S(1)}, u32[]{:S(2)}, u32[]{:S(2)}) collective-permute-start(bf16[96,768]{1,0:T(8,128)(2,1)} %get-tuple-element.52), channel_id=1, source_target_pairs={{0,4},{1,5},{2,6},{3,7},{4,12},{5,13},{6,14},{7,15},{8,0},{9,1},{1... | collective-permute-start | bytes 442376 | tf_op jit(solution)/shard_map/ppermute | solution.py:318
  16.7 8.9 %collective-permute-start.12 = (bf16[96,768]{1,0:T(8,128)(2,1)}, bf16[96,768]{1,0:T(8,128)(2,1)S(1)}, u32[]{:S(2)}, u32[]{:S(2)}) collective-permute-start(bf16[96,768]{1,0:T(8,128)(2,1)} %get-tuple-element.53), channel_id=1, source_target_pairs={{0,5},{1,4},{2,7},{3,6},{4,13},{5,12},{6,15},{7,14},{8,1},{9,0},{1... | collective-permute-start | bytes 442376 | tf_op jit(solution)/shard_map/ppermute | solution.py:318
  19.0 12.6 %collective-permute-start.13 = (bf16[96,768]{1,0:T(8,128)(2,1)}, bf16[96,768]{1,0:T(8,128)(2,1)S(1)}, u32[]{:S(2)}, u32[]{:S(2)}) collective-permute-start(bf16[96,768]{1,0:T(8,128)(2,1)} %get-tuple-element.54), channel_id=1, source_target_pairs={{0,6},{1,7},{2,4},{3,5},{4,14},{5,15},{6,12},{7,13},{8,2},{9,3},{1... | collective-permute-start | bytes 442376 | tf_op jit(solution)/shard_map/ppermute | solution.py:318
  21.0 13.0 %collective-permute-start.14 = (bf16[96,768]{1,0:T(8,128)(2,1)}, bf16[96,768]{1,0:T(8,128)(2,1)S(1)}, u32[]{:S(2)}, u32[]{:S(2)}) collective-permute-start(bf16[96,768]{1,0:T(8,128)(2,1)} %get-tuple-element.55), channel_id=1, source_target_pairs={{0,7},{1,6},{2,5},{3,4},{4,15},{5,14},{6,13},{7,12},{8,3},{9,2},{1... | collective-permute-start | bytes 442376 | tf_op jit(solution)/shard_map/ppermute | solution.py:318
  21.7 14.8 %collective-permute-start.8 = (bf16[96,768]{1,0:T(8,128)(2,1)}, bf16[96,768]{1,0:T(8,128)(2,1)S(1)}, u32[]{:S(2)}, u32[]{:S(2)}) collective-permute-start(bf16[96,768]{1,0:T(8,128)(2,1)} %get-tuple-element.49), channel_id=1, source_target_pairs={{0,1},{1,0},{2,3},{3,2},{4,5},{5,4},{6,7},{7,6},{8,9},{9,8},{10,11... | collective-permute-start | bytes 442376 | tf_op jit(solution)/shard_map/ppermute | solution.py:318
  24.2 12.7 %collective-permute-start.9 = (bf16[96,768]{1,0:T(8,128)(2,1)}, bf16[96,768]{1,0:T(8,128)(2,1)S(1)}, u32[]{:S(2)}, u32[]{:S(2)}) collective-permute-start(bf16[96,768]{1,0:T(8,128)(2,1)} %get-tuple-element.50), channel_id=1, source_target_pairs={{0,2},{1,3},{2,0},{3,1},{4,6},{5,7},{6,4},{7,5},{8,10},{9,11},{10,... | collective-permute-start | bytes 442376 | tf_op jit(solution)/shard_map/ppermute | solution.py:318
  25.7 14.2 %collective-permute-start.10 = (bf16[96,768]{1,0:T(8,128)(2,1)}, bf16[96,768]{1,0:T(8,128)(2,1)S(1)}, u32[]{:S(2)}, u32[]{:S(2)}) collective-permute-start(bf16[96,768]{1,0:T(8,128)(2,1)} %get-tuple-element.51), channel_id=1, source_target_pairs={{0,3},{1,2},{2,1},{3,0},{4,7},{5,6},{6,5},{7,4},{8,11},{9,10},{10,... | collective-permute-start | bytes 442376 | tf_op jit(solution)/shard_map/ppermute | solution.py:318
  31.5 8.3 %collective-permute-start.15 = (bf16[96,768]{1,0:T(8,128)(2,1)}, bf16[96,768]{1,0:T(8,128)(2,1)S(1)}, u32[]{:S(2)}, u32[]{:S(2)}) collective-permute-start(bf16[96,768]{1,0:T(8,128)(2,1)} %get-tuple-element.59), channel_id=1, source_target_pairs={{0,12},{1,13},{2,14},{3,15},{4,8},{5,9},{6,10},{7,11},{8,4},{9,5},... | collective-permute-start | bytes 442376 | tf_op jit(solution)/shard_map/ppermute | solution.py:318
  34.0 9.4 %collective-permute-start.16 = (bf16[96,768]{1,0:T(8,128)(2,1)}, bf16[96,768]{1,0:T(8,128)(2,1)S(1)}, u32[]{:S(2)}, u32[]{:S(2)}) collective-permute-start(bf16[96,768]{1,0:T(8,128)(2,1)} %get-tuple-element.60), channel_id=1, source_target_pairs={{0,13},{1,12},{2,15},{3,14},{4,9},{5,8},{6,11},{7,10},{8,5},{9,4},... | collective-permute-start | bytes 442376 | tf_op jit(solution)/shard_map/ppermute | solution.py:318
  36.5 22.9 %collective-permute-start.17 = (bf16[96,768]{1,0:T(8,128)(2,1)}, bf16[96,768]{1,0:T(8,128)(2,1)S(1)}, u32[]{:S(2)}, u32[]{:S(2)}) collective-permute-start(bf16[96,768]{1,0:T(8,128)(2,1)} %get-tuple-element.61), channel_id=1, source_target_pairs={{0,14},{1,15},{2,12},{3,13},{4,10},{5,11},{6,8},{7,9},{8,6},{9,7},... | collective-permute-start | bytes 442376 | tf_op jit(solution)/shard_map/ppermute | solution.py:318
  36.9 29.6 %collective-permute-start.18 = (bf16[96,768]{1,0:T(8,128)(2,1)}, bf16[96,768]{1,0:T(8,128)(2,1)S(1)}, u32[]{:S(2)}, u32[]{:S(2)}) collective-permute-start(bf16[96,768]{1,0:T(8,128)(2,1)} %get-tuple-element.62), channel_id=1, source_target_pairs={{0,15},{1,14},{2,13},{3,12},{4,11},{5,10},{6,9},{7,8},{8,7},{9,6},... | collective-permute-start | bytes 442376 | tf_op jit(solution)/shard_map/ppermute | solution.py:318
  39.9 26.6 %collective-permute-start.19 = (bf16[96,768]{1,0:T(8,128)(2,1)}, bf16[96,768]{1,0:T(8,128)(2,1)S(1)}, u32[]{:S(2)}, u32[]{:S(2)}) collective-permute-start(bf16[96,768]{1,0:T(8,128)(2,1)} %get-tuple-element.63), channel_id=1, source_target_pairs={{0,8},{1,9},{2,10},{3,11},{4,0},{5,1},{6,2},{7,3},{8,12},{9,13},{1... | collective-permute-start | bytes 442376 | tf_op jit(solution)/shard_map/ppermute | solution.py:318
  39.9 26.6 %collective-permute-start.20 = (bf16[96,768]{1,0:T(8,128)(2,1)}, bf16[96,768]{1,0:T(8,128)(2,1)S(1)}, u32[]{:S(2)}, u32[]{:S(2)}) collective-permute-start(bf16[96,768]{1,0:T(8,128)(2,1)} %get-tuple-element.64), channel_id=1, source_target_pairs={{0,9},{1,8},{2,11},{3,10},{4,1},{5,0},{6,3},{7,2},{8,13},{9,12},{1... | collective-permute-start | bytes 442376 | tf_op jit(solution)/shard_map/ppermute | solution.py:318
  43.4 23.1 %collective-permute-start.21 = (bf16[96,768]{1,0:T(8,128)(2,1)}, bf16[96,768]{1,0:T(8,128)(2,1)S(1)}, u32[]{:S(2)}, u32[]{:S(2)}) collective-permute-start(bf16[96,768]{1,0:T(8,128)(2,1)} %get-tuple-element.65), channel_id=1, source_target_pairs={{0,10},{1,11},{2,8},{3,9},{4,2},{5,3},{6,0},{7,1},{8,14},{9,15},{1... | collective-permute-start | bytes 442376 | tf_op jit(solution)/shard_map/ppermute | solution.py:318
  59.4 7.2 %collective-permute-start.22 = (bf16[96,768]{1,0:T(8,128)(2,1)}, bf16[96,768]{1,0:T(8,128)(2,1)S(1)}, u32[]{:S(2)}, u32[]{:S(2)}) collective-permute-start(bf16[96,768]{1,0:T(8,128)(2,1)} %get-tuple-element.66), channel_id=1, source_target_pairs={{0,11},{1,10},{2,9},{3,8},{4,3},{5,2},{6,1},{7,0},{8,15},{9,14},{1... | collective-permute-start | bytes 442376 | tf_op jit(solution)/shard_map/ppermute | solution.py:318
  70.6 12.6 %collective-permute-start.23 = (bf16[96,384]{1,0:T(8,128)(2,1)S(1)}, bf16[96,384]{1,0:T(8,128)(2,1)S(1)}, u32[]{:S(2)}, u32[]{:S(2)}) collective-permute-start(bf16[96,384]{1,0:T(8,128)(2,1)S(1)} %get-tuple-element.68), channel_id=1, source_target_pairs={{0,1},{1,0},{2,3},{3,2},{4,5},{5,4},{6,7},{7,6},{8,9},{9,8},{10,11... | collective-permute-start | bytes 221192 | tf_op jit(solution)/shard_map/ppermute | solution.py:318
  81.0 6.4 %collective-permute-start.27 = (bf16[96,384]{1,0:T(8,128)(2,1)S(1)}, bf16[96,384]{1,0:T(8,128)(2,1)S(1)}, u32[]{:S(2)}, u32[]{:S(2)}) collective-permute-start(bf16[96,384]{1,0:T(8,128)(2,1)S(1)} %get-tuple-element.72), channel_id=1, source_target_pairs={{0,5},{1,4},{2,7},{3,6},{4,1},{5,0},{6,3},{7,2},{8,13},{9,12},{10,... | collective-permute-start | bytes 221192 | tf_op jit(solution)/shard_map/ppermute | solution.py:318
  (17 other events, 120.2 us)
